TPU v7x, 256 devices: a whole 4x4x8 slice. The times are simulated.
256 devices in a mesh: mom: 64 (over z, y, core), tm: 4 (over x).
Axes of the slice: x: 4, y: 4, z: 8, core: 2. Of those that a mesh axis runs over, the one named last changes fastest.
Arguments:
- hist_lesser: float32 [2, 256, 16, 2048], P(None, 'mom', None, 'tm'), may hold values from -2 to 6
- hist_retarded: float32 [2, 256, 16, 2048], P(None, 'mom', None, 'tm'), may hold values from -4 to 4
- propagator: float32 [2, 256, 16, 16], P(None, 'mom'), may hold values from -0.5 to 1.5
- coupling: float32 [256], replicated, may hold values from 0.15 to 0.4
- mf_weight: float32 [256], replicated, may hold values from 0.5 to 2
- lag_weight: float32 [8], replicated, may hold values from 0.05 to 0.2
Outputs:
- new_slice: float32 [2, 256, 16, 2048], P(None, 'mom', None, 'tm')
All inputs are finite; a program needn't handle non-finite values.
Results may differ from a plain program's by a relative error of at most 0.0003.
Values sent between devices are 32-bit elements; how exact they have to be, the bound alone decides.
A program may use at most 64 MiB of HBM per device.

v0:
```python
import math

import jax
import jax.numpy as jnp
from jax import lax
from jax.sharding import PartitionSpec as P

KX = 16
KY = 16
ORB = 16
W = 8
PASSES = 3


HIGHEST = lax.Precision.HIGHEST


def shifted(x, axis, by):
    peers = lax.axis_size(axis)
    pairs = [(i, i + by) for i in range(peers) if 0 <= i + by < peers]
    return lax.ppermute(x, axis, pairs)


def broadcast(x, axis, root):
    mine = lax.axis_index(axis) == root
    return lax.psum(jnp.where(mine, x, jnp.zeros_like(x)), axis)


def momentum_tables():
    index = jnp.arange(KX * KY, dtype=jnp.int32)
    first = index // KY
    second = index % KY
    turn_x = first[:, None] * first[None, :] % KX
    turn_y = second[:, None] * second[None, :] % KY
    phase = 2.0 * math.pi * (turn_x.astype(jnp.float32) / KX + turn_y.astype(jnp.float32) / KY)
    scale = 1.0 / math.sqrt(KX * KY)
    return (jnp.cos(phase) * scale, jnp.sin(phase) * scale)


def complex_product(pattern, first, second):
    real = jnp.einsum(pattern, first[0], second[0], precision=HIGHEST) - jnp.einsum(
        pattern, first[1], second[1], precision=HIGHEST
    )
    imaginary = jnp.einsum(pattern, first[0], second[1], precision=HIGHEST) + jnp.einsum(
        pattern, first[1], second[0], precision=HIGHEST
    )
    return jnp.stack([real, imaginary])


def back_to_momenta(real, imaginary, cosine, sine):
    out_real = jnp.dot(cosine, real, precision=HIGHEST) + jnp.dot(
        sine, imaginary, precision=HIGHEST
    )
    out_imag = jnp.dot(cosine, imaginary, precision=HIGHEST) - jnp.dot(
        sine, real, precision=HIGHEST
    )
    return jnp.stack([out_real, out_imag])


def local_products(arrived, cosine, sine, strength, lag_mark):
    lag_count = lag_mark.shape[0]
    space_real = jnp.dot(cosine, arrived[0], precision=HIGHEST) - jnp.dot(
        sine, arrived[1], precision=HIGHEST
    )
    space_imag = jnp.dot(cosine, arrived[1], precision=HIGHEST) + jnp.dot(
        sine, arrived[0], precision=HIGHEST
    )
    column_strength = jnp.repeat(strength, lag_count)
    magnitude = column_strength * (space_real * space_real + space_imag * space_imag)
    lesser_real = magnitude * space_real
    lesser_imag = magnitude * space_imag
    pair_real = column_strength * (space_real * space_real - space_imag * space_imag)
    pair_imag = column_strength * 2.0 * space_real * space_imag
    return (
        back_to_momenta(lesser_real, lesser_imag, cosine, sine),
        back_to_momenta(pair_real, pair_imag, cosine, sine),
    )


def self_energies(window, cosine, sine, strength, mf_weight, last_mark):
    momenta_here = window.shape[1]
    outgoing = window.reshape(2, momenta_here, ORB * ORB * W)
    arrived = lax.all_to_all(outgoing, "mom", split_axis=2, concat_axis=1, tiled=True)
    lesser_r, pair_r = local_products(arrived, cosine, sine, strength, last_mark)
    back_lesser, back_pair = (
        lax.all_to_all(lesser_r, "mom", split_axis=1, concat_axis=2, tiled=True),
        lax.all_to_all(pair_r, "mom", split_axis=1, concat_axis=2, tiled=True),
    )
    sigma = back_lesser.reshape(2, momenta_here, ORB, ORB, W)
    pair_k = back_pair.reshape(2, momenta_here, ORB, ORB, W)
    own_total = jnp.sum(window[..., W - 1], axis=1)
    occupation = lax.psum(own_total, "mom") / (KX * KY)
    sigma = sigma + (mf_weight.reshape(ORB, ORB) * occupation)[:, None, :, :, None] * last_mark
    return (sigma, pair_k)


def collide(sigma, pair_k, lag_weight, padded_r, padded_l, count):
    weighted_sigma = sigma * lag_weight
    weighted_pair = pair_k * lag_weight

    def ladder(padded):
        return jnp.stack(
            [padded[..., offset * ORB : (offset + count) * ORB] for offset in range(W)], axis=3
        )

    return complex_product("kabm,kbmx->kax", weighted_sigma, ladder(padded_r)) + complex_product(
        "kabm,kbmx->kax", weighted_pair, ladder(padded_l)
    )


def on_device(hist_lesser, hist_retarded, propagator, coupling, mf_weight, lag_weight):
    momenta_here = hist_lesser.shape[1]
    times_here = hist_lesser.shape[3] // ORB
    cosine, sine = momentum_tables()
    lesser = hist_lesser.reshape(2, momenta_here, ORB, times_here, ORB)
    start = complex_product("kab,kbjc->kajc", propagator, lesser).reshape(
        2, momenta_here, ORB, times_here * ORB
    )
    rim_width = (W - 1) * ORB
    rim_retarded, rim_lesser = shifted(
        (
            hist_retarded[..., times_here * ORB - rim_width :],
            hist_lesser[..., times_here * ORB - rim_width :],
        ),
        "tm",
        1,
    )
    padded_r = jnp.concatenate([rim_retarded, hist_retarded], axis=3)
    padded_l = jnp.concatenate([rim_lesser, hist_lesser], axis=3)
    block = min(32, times_here)
    count_blocks = times_here // block
    window_start = (times_here - W) * ORB
    pair_count = ORB * ORB // lax.axis_size("mom")
    strength = lax.dynamic_slice_in_dim(
        coupling * coupling, lax.axis_index("mom") * pair_count, pair_count, 0
    )
    last_mark = (jnp.arange(W) == W - 1).astype(jnp.float32)
    owner = lax.axis_size("tm") - 1
    current = start[..., window_start:]
    full_slice = start
    for sweep in range(PASSES):
        shared = broadcast(current, "tm", owner)
        window = jnp.transpose(shared.reshape(2, momenta_here, ORB, W, ORB), (0, 1, 2, 4, 3))
        sigma, pair_k = self_energies(window, cosine, sine, strength, mf_weight, last_mark)
        blocks_out = lax.map(
            lambda number: collide(sigma, pair_k, lag_weight, padded_r, padded_l, block),
            jnp.arange(count_blocks, dtype=jnp.int32),
        )
        collision = jnp.moveaxis(blocks_out, 0, 3).reshape(2, momenta_here, ORB, times_here * ORB)
        full_slice = start + jnp.stack([collision[1], -collision[0]])
        current = full_slice[..., window_start:]
    return full_slice


def solution(mesh):
    return jax.shard_map(
        on_device,
        mesh=mesh,
        in_specs=(
            P(None, "mom", None, "tm"),
            P(None, "mom", None, "tm"),
            P(None, "mom", None, None),
            P(),
            P(),
            P(),
        ),
        out_specs=P(None, "mom", None, "tm"),
        check_vma=False,
    )
```

profile of v0, /device:TPU:1, one launch (start us, length us, event | category | flops | bytes accessed | tf_op | source)
XLA Modules:
  0.0 1244.2 jit_solution(204335925724483191)
XLA Ops:
  32.2 42.9 %all-reduce.4.cloned.1.call-done = f32[2,4,16,16,8]{4,3,2,1,0:T(8,128)} async-done(((f32[2,4,16,16,8]{4,3,2,1,0:T(8,128)}), f32[2,4,16,16,8]{4,3,2,1,0:T(8,128)}) %all-reduce.4.cloned.1.call-update) | async-done | bytes 65552 | tf_op jit(solution)/shard_map/psum | solution.py:26
  76.8 246.1 %psum.43 = f32[2,16,16]{2,1,0:T(8,128)S(1)} all-reduce(f32[2,16,16]{2,1,0:T(8,128)S(1)} %slice_reduce_fusion.2), channel_id=1, replica_groups=mesh['mom'=64,'tm'=4] {'mom'}, use_global_device_ids=true, to_apply=%region_2.3 | all-reduce | flops 512 | bytes 4096 | tf_op jit(solution)/shard_map/psum | solution.py:92
  322.9 5.3 copy.147
  328.2 4.8 reshape.187
  333.0 10.4 all-to-all-start
  343.4 10.1 all-to-all-done
  355.0 4.6 reshape.188
  388.0 7.5 all-to-all-done.1
  395.4 4.4 all-to-all-start.2
  402.3 7.7 all-to-all-done.2
  434.1 43.3 %all-reduce.6.cloned.1.call-done = f32[2,4,16,16,8]{4,3,2,1,0:T(8,128)} async-done(((f32[2,4,16,16,8]{4,3,2,1,0:T(8,128)}), f32[2,4,16,16,8]{4,3,2,1,0:T(8,128)}) %all-reduce.6.cloned.1.call-update) | async-done | bytes 65552 | tf_op jit(solution)/shard_map/psum | solution.py:26
  479.1 246.2 %psum.45 = f32[2,16,16]{2,1,0:T(8,128)S(1)} all-reduce(f32[2,16,16]{2,1,0:T(8,128)S(1)} %slice_reduce_fusion.1), channel_id=1, replica_groups=mesh['mom'=64,'tm'=4] {'mom'}, use_global_device_ids=true, to_apply=%region_5.6 | all-reduce | flops 512 | bytes 4096 | tf_op jit(solution)/shard_map/psum | solution.py:92
  725.4 5.3 copy.149
  730.7 4.8 reshape.193
  735.5 10.4 all-to-all-start.3
  745.9 10.1 all-to-all-done.3
  756.9 4.6 reshape.194
  782.9 4.4 all-to-all-start.4
  789.9 7.5 all-to-all-done.4
  797.4 4.4 all-to-all-start.5
  804.0 8.0 all-to-all-done.5
  836.1 43.3 %all-reduce.8.cloned.1.call-done = f32[2,4,16,16,8]{4,3,2,1,0:T(8,128)} async-done(((f32[2,4,16,16,8]{4,3,2,1,0:T(8,128)}), f32[2,4,16,16,8]{4,3,2,1,0:T(8,128)}) %all-reduce.8.cloned.1.call-update) | async-done | bytes 65552 | tf_op jit(solution)/shard_map/psum | solution.py:26
  881.1 246.5 %psum.47 = f32[2,16,16]{2,1,0:T(8,128)S(1)} all-reduce(f32[2,16,16]{2,1,0:T(8,128)S(1)} %slice_reduce_fusion), channel_id=1, replica_groups=mesh['mom'=64,'tm'=4] {'mom'}, use_global_device_ids=true, to_apply=%region_8.9 | all-reduce | flops 512 | bytes 4096 | tf_op jit(solution)/shard_map/psum | solution.py:92
  1127.5 5.3 copy.151
  1132.9 4.8 reshape.199
  1137.7 10.4 all-to-all-start.6
  1148.1 10.1 all-to-all-done.6
  1159.1 4.6 reshape.200
  1184.9 4.4 all-to-all-start.7
  1191.9 7.5 all-to-all-done.7
  1199.4 4.8 all-to-all-start.8
  1206.1 8.1 all-to-all-done.8
  (247 shorter events, 186.9 us)
Async XLA Ops:
  6.5 68.6 %all-reduce.4.cloned.1.call-start = ((), (), s32[]{:S(2)}) async-start(), calls=%async_computation.9 | async-start | bytes 2097152 | tf_op jit(solution)/shard_map/psum | solution.py:26
  7.5 17.9 %collective-permute-start.1 = (f32[2,4,16,112]{3,2,1,0:T(8,128)S(1)}, f32[2,4,16,112]{3,2,1,0:T(8,128)S(1)}, u32[]{:S(2)}, u32[]{:S(2)}) collective-permute-start(f32[2,4,16,112]{3,2,1,0:T(8,128)S(1)} %slice.330), channel_id=1, source_target_pairs={{0,1},{1,2},{2,3},{4,5},{5,6},{6,7},{8,9},{9,10},{10,11},{12,13},{... | collective-permute-start | bytes 172040 | tf_op jit(solution)/shard_map/ppermute | solution.py:21
  12.3 11.9 collective-permute-start
  16.8 1.1 copy-start.2
  22.2 1.7 copy-start.4
  22.2 1.7 copy-start.5
  22.2 2.0 copy-start.1
  23.8 361.5 %copy-start.6 = (s32[256]{0:T(256)}, s32[256]{0:T(256)S(1)}, u32[]{:S(2)}) copy-start(s32[256]{0:T(256)S(1)} %get-tuple-element.95) | copy-start | bytes 3076
  23.8 361.5 %copy-start.9 = (s32[256]{0:T(256)}, s32[256]{0:T(256)S(1)}, u32[]{:S(2)}) copy-start(s32[256]{0:T(256)S(1)} %get-tuple-element.96) | copy-start | bytes 3076
  24.1 354.2 %copy-start.12 = (f32[32]{0:T(128)}, f32[32]{0:T(128)S(1)}, u32[]{:S(2)}) copy-start(f32[32]{0:T(128)S(1)} %mul.866) | copy-start | bytes 388
  24.1 361.2 %copy-start.15 = (f32[32]{0:T(128)}, f32[32]{0:T(128)S(1)}, u32[]{:S(2)}) copy-start(f32[32]{0:T(128)S(1)} %broadcast_multiply_fusion.10) | copy-start | bytes 388
  24.4 1.0 copy-start
  333.0 20.5 %all-to-all-start = ((f32[64,1,256]{2,1,0:T(1,128)}), f32[64,1,256]{2,1,0:T(1,128)S(1)}, u32[]{:S(2)}, u32[]{:S(2)}) async-start(f32[64,1,256]{2,1,0:T(1,128)} %reshape.187), calls=%async_computation | async-start | bytes 131072 | tf_op jit(solution)/shard_map/all_to_all | solution.py:83
  380.9 14.5 %all-to-all-start.1 = ((f32[64,1,256]{2,1,0:T(1,128)}), f32[64,1,256]{2,1,0:T(1,128)S(1)}, u32[]{:S(2)}, u32[]{:S(2)}) async-start(f32[64,1,256]{2,1,0:T(1,128)} %reshape.189), calls=%async_computation.1 | async-start | bytes 131072 | tf_op jit(solution)/shard_map/all_to_all | solution.py:86
  395.4 14.6 %all-to-all-start.2 = ((f32[64,1,256]{2,1,0:T(1,128)}), f32[64,1,256]{2,1,0:T(1,128)S(1)}, u32[]{:S(2)}, u32[]{:S(2)}) async-start(f32[64,1,256]{2,1,0:T(1,128)} %reshape.191), calls=%async_computation.2 | async-start | bytes 131072 | tf_op jit(solution)/shard_map/all_to_all | solution.py:87
  399.9 77.6 %all-reduce.6.cloned.1.call-start = ((), (), s32[]{:S(2)}) async-start(), calls=%async_computation.10 | async-start | bytes 2097152 | tf_op jit(solution)/shard_map/psum | solution.py:26
  413.1 3.5 copy-start.3
  735.5 20.5 %all-to-all-start.3 = ((f32[64,1,256]{2,1,0:T(1,128)}), f32[64,1,256]{2,1,0:T(1,128)S(1)}, u32[]{:S(2)}, u32[]{:S(2)}) async-start(f32[64,1,256]{2,1,0:T(1,128)} %reshape.193), calls=%async_computation.3 | async-start | bytes 131072 | tf_op jit(solution)/shard_map/all_to_all | solution.py:83
  761.4 3.1 copy-start.7
  761.4 3.1 copy-start.10
  767.7 3.1 copy-start.13
  769.2 3.1 copy-start.16
  782.9 14.5 %all-to-all-start.4 = ((f32[64,1,256]{2,1,0:T(1,128)}), f32[64,1,256]{2,1,0:T(1,128)S(1)}, u32[]{:S(2)}, u32[]{:S(2)}) async-start(f32[64,1,256]{2,1,0:T(1,128)} %reshape.195), calls=%async_computation.4 | async-start | bytes 131072 | tf_op jit(solution)/shard_map/all_to_all | solution.py:86
  797.4 14.6 %all-to-all-start.5 = ((f32[64,1,256]{2,1,0:T(1,128)}), f32[64,1,256]{2,1,0:T(1,128)S(1)}, u32[]{:S(2)}, u32[]{:S(2)}) async-start(f32[64,1,256]{2,1,0:T(1,128)} %reshape.197), calls=%async_computation.5 | async-start | bytes 131072 | tf_op jit(solution)/shard_map/all_to_all | solution.py:87
  801.9 77.5 %all-reduce.8.cloned.1.call-start = ((), (), s32[]{:S(2)}) async-start(), calls=%async_computation.11 | async-start | bytes 2097152 | tf_op jit(solution)/shard_map/psum | solution.py:26
  1137.7 20.5 %all-to-all-start.6 = ((f32[64,1,256]{2,1,0:T(1,128)}), f32[64,1,256]{2,1,0:T(1,128)S(1)}, u32[]{:S(2)}, u32[]{:S(2)}) async-start(f32[64,1,256]{2,1,0:T(1,128)} %reshape.199), calls=%async_computation.6 | async-start | bytes 131072 | tf_op jit(solution)/shard_map/all_to_all | solution.py:83
  1163.6 3.1 copy-start.8
  1163.6 3.1 copy-start.11
  1169.9 3.1 copy-start.14
  1171.4 3.1 copy-start.17
  1184.9 14.5 %all-to-all-start.7 = ((f32[64,1,256]{2,1,0:T(1,128)}), f32[64,1,256]{2,1,0:T(1,128)S(1)}, u32[]{:S(2)}, u32[]{:S(2)}) async-start(f32[64,1,256]{2,1,0:T(1,128)} %reshape.201), calls=%async_computation.7 | async-start | bytes 131072 | tf_op jit(solution)/shard_map/all_to_all | solution.py:86
  1199.4 14.8 %all-to-all-start.8 = ((f32[64,1,256]{2,1,0:T(1,128)}), f32[64,1,256]{2,1,0:T(1,128)S(1)}, u32[]{:S(2)}, u32[]{:S(2)}) async-start(f32[64,1,256]{2,1,0:T(1,128)} %reshape.203), calls=%async_computation.8 | async-start | bytes 131072 | tf_op jit(solution)/shard_map/all_to_all | solution.py:87
Sparse Core Ops, SparseCore 0:
  23.9 51.1 all-reduce.3
  434.2 43.1 all-reduce.5
  836.2 43.1 all-reduce.7
where the time goes:
time: 1260 us; the launch traced here: 1240 us
  blocking collectives  739 us (59%)
  waiting for transfers between devices  206 us (16%)
  matrix products  101 us (8%)
  local copies, waits for them, and re-layouts  92.5 us (7%)
  starting transfers between devices  65.9 us (5%)
  other arithmetic  25.2 us (2%)
  between operations  14.7 us (1%)
    psum x3, blocking collectives, self_energies(): occupation = lax.psum(own_total, 'mom') / (KX * KY)  739 us
    psum x3, waiting for transfers between devices, broadcast(): return lax.psum(jnp.where(mine, x, jnp.zeros_like(x)), axis)  130 us
    unnamed x55, local copies, waits for them, and re-layouts  35 us
    all_to_all x3, starting transfers between devices, self_energies(): lax.all_to_all(outgoing, 'mom', split_axis=2, concat_axis=1, tiled=True)  31.3 us
    all_to_all x3, waiting for transfers between devices, self_energies(): lax.all_to_all(outgoing, 'mom', split_axis=2, concat_axis=1, tiled=True)  30.2 us
  transfers between devices with their start and end apart: 14, of which 12 were waited for; matrix products, arithmetic and copies ran while one was open for 2% of the time, Pallas kernels for 0%

commit v1 on v0

v1 whole, which is shorter than its diff:
```python
import functools
import math

import jax
import jax.numpy as jnp
import ml_dtypes
import numpy as np
from jax import lax
from jax.experimental import pallas as pl
from jax.experimental.pallas import tpu as pltpu
from jax.sharding import PartitionSpec as P

KX = 16
KY = 16
ORB = 16
W = 8
PASSES = 3
NZ, NY = 8, 4
CHIPS = NZ * NY
TM = 4
HERE = 4
LANES = W * ORB
HALF = LANES // 2
BLOCKS = 4

MESH = pl.DeviceIdType.MESH
F32 = jnp.float32
BF16 = jnp.bfloat16


def momentum_table():
    place = np.arange(KX * KY)
    core, chip, here = place // 128, place // 4 % 32, place % 4
    k = 8 * chip + 4 * core + here
    kx, ky = k // KY, k % KY
    turn = (kx[:, None] * kx[None, :]) % KX + (ky[:, None] * ky[None, :]) % KY
    phase = 2.0 * math.pi * turn / 16.0
    full = np.concatenate([np.cos(phase), np.sin(phase)], axis=1) / 16.0
    full = full.astype(np.float32)
    high = full.astype(ml_dtypes.bfloat16)
    low = (full - high.astype(np.float32)).astype(ml_dtypes.bfloat16)
    return np.stack([high, low])


def split(x):
    high = x.astype(BF16)
    return high, (x - high.astype(F32)).astype(BF16)


def mm(a, b):
    return jnp.dot(a, b, preferred_element_type=F32)


def kernel(
    hl, hr, prop, coup, mf, lag, table,
    out,
    hlv, hrv, wl, wr, tab, startv, startw, hank, sendf, fbuf, sendb, rbuf,
    load_sem, x_send, x_recv, f_send, f_recv, f_own, s_send, s_recv, b_send, b_recv,
):
    dev = lax.axis_index("mom")
    x = lax.axis_index("tm")
    core = lax.rem(dev, 2)
    chip = dev // 2
    z = chip // NY
    y = lax.rem(chip, NY)
    row = chip // 2
    half = lax.rem(chip, 2)

    def peer_chip(dz, dy):
        return lax.rem(z + dz, NZ) * NY + lax.rem(y + dy, NY)

    offsets = [(dz, dy) for dz in (4, 3, 5, 2, 6, 1, 7, 0) for dy in (2, 1, 3, 0) if dz or dy]

    barrier = pltpu.get_barrier_semaphore()
    for dx in (1, 2, 3):
        pl.semaphore_signal(
            barrier, inc=1, device_id={"mom": dev, "tm": lax.rem(x + dx, TM)}, device_id_type=MESH
        )
    for dz, dy in offsets:
        pl.semaphore_signal(
            barrier, inc=1, device_id={"mom": peer_chip(dz, dy) * 2 + core, "tm": x},
            device_id_type=MESH,
        )
    pl.semaphore_signal(
        barrier, inc=1, device_id={"mom": chip * 2 + 1 - core, "tm": x}, device_id_type=MESH
    )

    loads = [
        pltpu.make_async_copy(hl, hlv.at[:, :, :, pl.ds(LANES, BLOCKS * LANES)], load_sem.at[0]),
        pltpu.make_async_copy(hr, hrv.at[:, :, :, pl.ds(LANES, BLOCKS * LANES)], load_sem.at[1]),
        pltpu.make_async_copy(table, tab, load_sem.at[2]),
    ]
    for load in loads:
        load.start()

    own_window = [
        pltpu.make_async_copy(hl.at[:, :, :, pl.ds(2 * LANES, 2 * LANES)], wl, load_sem.at[3]),
        pltpu.make_async_copy(hr.at[:, :, :, pl.ds(2 * LANES, 2 * LANES)], wr, load_sem.at[4]),
    ]

    @pl.when(x == TM - 1)
    def _():
        for copy in own_window:
            copy.start()

    pl.semaphore_wait(barrier, len(offsets) + 4)

    def window_copy(part, target, slot):
        src, dst = (
            (hl.at[:, :, :, pl.ds(3 * LANES, LANES)], wl.at[:, :, :, pl.ds(LANES, LANES)]),
            (hl.at[:, :, :, pl.ds(2 * LANES, LANES)], wl.at[:, :, :, pl.ds(0, LANES)]),
            (hr.at[:, :, :, pl.ds(2 * LANES, 2 * LANES)], wr),
        )[part]
        return pltpu.make_async_remote_copy(
            src_ref=src, dst_ref=dst, send_sem=x_send.at[part, slot], recv_sem=x_recv.at[part],
            device_id={"mom": dev, "tm": target}, device_id_type=MESH,
        )

    def rim_copy(part):
        src, dst = ((hl, hlv), (hr, hrv))[part]
        return pltpu.make_async_remote_copy(
            src_ref=src.at[:, :, :, pl.ds(3 * LANES, LANES)],
            dst_ref=dst.at[:, :, :, pl.ds(0, LANES)],
            send_sem=x_send.at[3 + part, 0], recv_sem=x_recv.at[3 + part],
            device_id={"mom": dev, "tm": lax.rem(x + 1, TM)}, device_id_type=MESH,
        )

    @pl.when(x == TM - 1)
    def _():
        for part in range(3):
            for slot, target in enumerate((1, 0, 2)):
                window_copy(part, target, slot).start()

    @pl.when(x < TM - 1)
    def _():
        for part in range(2):
            rim_copy(part).start()

    @pl.when(x == 0)
    def _():
        zeros = jnp.zeros((2, HERE, ORB, LANES), F32)
        hlv[:, :, :, pl.ds(0, LANES)] = zeros
        hrv[:, :, :, pl.ds(0, LANES)] = zeros

    lane = lax.broadcasted_iota(jnp.int32, (1, LANES), 1)
    low_half = lane < HALF
    sign = jnp.where(low_half, -1.0, 1.0).astype(F32)

    coup_lane = jnp.zeros((1, LANES), F32)
    mf_lane = jnp.zeros((1, LANES), F32)
    for b in range(ORB):
        here = lax.rem(lane, ORB) == b
        coup_lane = jnp.where(here, coup[row * ORB + b], coup_lane)
        mf_lane = jnp.where(here, mf[row * ORB + b], mf_lane)
    strength = coup_lane * coup_lane
    newest = (lax.rem(lane, HALF) >= HALF - ORB) & (half == 1)
    mf_lane = jnp.where(newest, mf_lane, 0.0)
    first_row = lax.broadcasted_iota(jnp.int32, (KX * KY, 1), 0) == 0
    mf_term = jnp.where(first_row, mf_lane, 0.0)
    low_rows = lax.broadcasted_iota(jnp.int32, (1, 8, 1), 1) < 4

    def propagate(k, source, lanes_from, count):
        stack = jnp.concatenate([prop[0, k], prop[1, k]], axis=0)
        real = jnp.dot(
            stack, source[0, k, :, pl.ds(lanes_from, count)],
            precision=lax.Precision.HIGHEST, preferred_element_type=F32,
        )
        imag = jnp.dot(
            stack, source[1, k, :, pl.ds(lanes_from, count)],
            precision=lax.Precision.HIGHEST, preferred_element_type=F32,
        )
        return real[:ORB] - imag[ORB:], real[ORB:] + imag[:ORB]

    def build(k, slot, source_r, source_l, lanes_from):
        for lp, source in enumerate((source_r, source_l)):
            for c in range(2):
                first = source[c, k, :, pl.ds(lanes_from, LANES)]
                second = source[c, k, :, pl.ds(lanes_from + LANES, LANES)]
                for m in range(W):
                    shift = ORB * (m + 1)
                    if shift < LANES:
                        moved = pltpu.roll(
                            jnp.where(lane >= shift, first, second), LANES - shift, 1
                        )
                    else:
                        moved = second
                    high, low = split(moved * lag[m])
                    at = lp * LANES + m * ORB
                    hank[slot, 0, pl.ds(at, ORB), pl.ds(c * LANES, LANES)] = high
                    hank[slot, 1, pl.ds(at, ORB), pl.ds(c * LANES, LANES)] = low

    def send_window(p, k, real, imag):
        turned_real = pltpu.roll(real, HALF, 1)
        turned_imag = pltpu.roll(imag, HALF, 1)
        sendf[p, 0, pl.ds(k, ORB, stride=HERE), :] = jnp.where(low_half, real, turned_imag)
        sendf[p, 1, pl.ds(k, ORB, stride=HERE), :] = jnp.where(low_half, turned_real, imag)

    def forward_copy(p, target):
        return pltpu.make_async_remote_copy(
            src_ref=sendf.at[p, lax.rem(target, 2), pl.ds((target // 2) * HERE, HERE), :],
            dst_ref=fbuf.at[p, pl.ds((core * CHIPS + chip) * HERE, HERE), :],
            send_sem=f_send.at[p], recv_sem=f_recv.at[p],
            device_id={"mom": target * 2 + core, "tm": x}, device_id_type=MESH,
        )

    def back_copy(p, target):
        return pltpu.make_async_remote_copy(
            src_ref=sendb.at[p, target],
            dst_ref=rbuf.at[p, half, pl.ds(row * 8, 8), :],
            send_sem=b_send.at[p], recv_sem=b_recv.at[p],
            device_id={"mom": target * 2 + core, "tm": x}, device_id_type=MESH,
        )

    def pair_copy(p):
        block = fbuf.at[p, pl.ds(core * CHIPS * HERE, CHIPS * HERE), :]
        return pltpu.make_async_remote_copy(
            src_ref=block, dst_ref=block, send_sem=s_send.at[p], recv_sem=s_recv.at[p],
            device_id={"mom": chip * 2 + 1 - core, "tm": x}, device_id_type=MESH,
        )

    def arrived(p, k):
        columns = []
        for lp in range(2):
            first = rbuf[p, 0, pl.ds(lp * HERE + k, ORB, stride=8), :]
            second = rbuf[p, 1, pl.ds(lp * HERE + k, ORB, stride=8), :]
            real = jnp.where(low_half, first, pltpu.roll(second, HALF, 1))
            imag = jnp.where(low_half, pltpu.roll(first, HALF, 1), second)
            columns.append(jnp.concatenate([real, imag], axis=0))
        high, low = split(jnp.concatenate(columns, axis=1))
        return jnp.concatenate([high, low], axis=0)

    def collide(stack, slot):
        rows = 2 * ORB
        product = mm(stack, hank[slot, 0])
        total = product[:rows] + product[rows:] + mm(stack[:rows], hank[slot, 1])
        real = total[:ORB, :LANES] - total[ORB:, LANES:]
        imag = total[:ORB, LANES:] + total[ORB:, :LANES]
        return real, imag

    @pl.when(x == TM - 1)
    def _():
        for copy in own_window:
            copy.wait()

    @pl.when(x < TM - 1)
    def _():
        window_copy(0, 0, 0).wait_recv()

    for k in range(HERE):
        real, imag = propagate(k, wl, LANES, LANES)
        startw[0, k] = real
        startw[1, k] = imag
        send_window(0, k, real, imag)

    for p in range(PASSES):
        own = pltpu.make_async_copy(
            sendf.at[p, half, pl.ds(row * HERE, HERE), :],
            fbuf.at[p, pl.ds((core * CHIPS + chip) * HERE, HERE), :],
            f_own.at[p],
        )
        own.start()
        for dz, dy in offsets:
            forward_copy(p, peer_chip(dz, dy)).start()

        if p == 0:
            @pl.when(x < TM - 1)
            def _():
                window_copy(1, 0, 0).wait_recv()
                window_copy(2, 0, 0).wait_recv()

            for k in range(HERE):
                build(k, BLOCKS * HERE + k, wr, wl, 0)
            for load in loads:
                load.wait()

            @pl.when(x > 0)
            def _():
                for part in range(2):
                    rim_copy(part).wait_recv()
        else:
            for k in range(HERE):
                for block in (2 * (p - 1), 2 * (p - 1) + 1):
                    build(k, block * HERE + k, hrv, hlv, block * LANES)

        own.wait()
        landed = fbuf.at[p, pl.ds(0, (CHIPS - 1) * HERE), :]
        pltpu.make_async_copy(landed, landed, f_recv.at[p]).wait()
        pair_copy(p).start()
        pair_copy(p).wait_recv()

        here = fbuf[p]
        high, low = split(jnp.concatenate([here, pltpu.roll(here, HALF, 1) * sign], axis=0))
        both = mm(tab[0], jnp.concatenate([high, low], axis=1))
        pos = both[:, :LANES] + both[:, LANES:] + mm(tab[1], high)
        turned = pltpu.roll(pos, HALF, 1)
        square = pos * pos
        turned_square = pltpu.roll(square, HALF, 1)
        lesser = (strength * (square + turned_square) + mf_term) * pos
        pair = strength * jnp.where(low_half, square - turned_square, 2.0 * pos * turned)
        both = jnp.concatenate([lesser, pair], axis=1)
        other = jnp.concatenate(
            [pltpu.roll(lesser, HALF, 1) * -sign, pltpu.roll(pair, HALF, 1) * -sign], axis=1
        )
        high, low = split(jnp.concatenate([both, other], axis=0))
        mine = pl.ds(pl.multiple_of(core * (CHIPS * HERE), CHIPS * HERE), CHIPS * HERE)
        tab_high, tab_low = tab[0, mine, :], tab[1, mine, :]
        back = mm(tab_high, high) + mm(tab_high, low) + mm(tab_low, high)
        left = back[:, :LANES].reshape(CHIPS // 2, 8, LANES)
        right = back[:, LANES:].reshape(CHIPS // 2, 8, LANES)
        even = jnp.where(low_rows, left, pltpu.roll(right, 4, 1))
        odd = jnp.where(low_rows, pltpu.roll(left, 4, 1), right)
        for pair_index in range(CHIPS // 2):
            sendb[p, 2 * pair_index] = even[pair_index]
            sendb[p, 2 * pair_index + 1] = odd[pair_index]
        rbuf[p, half, pl.ds(pl.multiple_of(row * 8, 8), 8), :] = sendb[p, chip]
        for dz, dy in offsets:
            back_copy(p, peer_chip(dz, dy)).start()

        if p == 0:
            for k in range(HERE):
                real, imag = propagate(k, hlv, LANES, BLOCKS * LANES)
                startv[0, k] = real
                startv[1, k] = imag

        landed = sendb.at[p, pl.ds(0, CHIPS - 1)]
        pltpu.make_async_copy(landed, landed, b_recv.at[p]).wait()

        if p < PASSES - 1:
            for k in range(HERE):
                real, imag = collide(arrived(p, k), BLOCKS * HERE + k)
                send_window(p + 1, k, startw[0, k] + imag, startw[1, k] - real)
        else:
            for k in range(HERE):
                stack = arrived(p, k)
                for block in range(BLOCKS):
                    real, imag = collide(stack, block * HERE + k)
                    at = pl.ds(block * LANES, LANES)
                    out[0, k, :, at] = startv[0, k, :, at] + imag
                    out[1, k, :, at] = startv[1, k, :, at] - real

    for p in range(PASSES):
        sent = fbuf.at[p, pl.ds(0, (CHIPS - 1) * HERE), :]
        pltpu.make_async_copy(sent, sent, f_send.at[p]).wait()
        sent = sendb.at[p, pl.ds(0, CHIPS - 1)]
        pltpu.make_async_copy(sent, sent, b_send.at[p]).wait()
        pair_copy(p).wait_send()

    @pl.when(x == TM - 1)
    def _():
        for part in range(3):
            for slot in range(3):
                window_copy(part, slot, slot).wait_send()

    @pl.when(x < TM - 1)
    def _():
        for part in range(2):
            rim_copy(part).wait_send()


def on_device(table, hist_lesser, hist_retarded, propagator, coupling, mf_weight, lag_weight):
    vmem = pl.BlockSpec(memory_space=pltpu.VMEM)
    smem = pl.BlockSpec(memory_space=pltpu.SMEM)
    anywhere = pl.BlockSpec(memory_space=pl.ANY)
    padded = (2, HERE, ORB, (BLOCKS + 1) * LANES)
    return pl.pallas_call(
        kernel,
        out_shape=jax.ShapeDtypeStruct(hist_lesser.shape, F32),
        in_specs=[anywhere, anywhere, vmem, smem, smem, smem, anywhere],
        out_specs=vmem,
        scratch_shapes=[
            pltpu.VMEM(padded, F32),
            pltpu.VMEM(padded, F32),
            pltpu.VMEM((2, HERE, ORB, 2 * LANES), F32),
            pltpu.VMEM((2, HERE, ORB, 2 * LANES), F32),
            pltpu.VMEM((2, KX * KY, 2 * KX * KY), BF16),
            pltpu.VMEM((2, HERE, ORB, BLOCKS * LANES), F32),
            pltpu.VMEM((2, HERE, ORB, LANES), F32),
            pltpu.VMEM(((BLOCKS + 1) * HERE, 2, 2 * LANES, 2 * LANES), BF16),
            pltpu.VMEM((PASSES, 2, ORB * HERE, LANES), F32),
            pltpu.VMEM((PASSES, KX * KY, LANES), F32),
            pltpu.VMEM((PASSES, CHIPS, 8, LANES), F32),
            pltpu.VMEM((PASSES, 2, ORB * 8, LANES), F32),
            pltpu.SemaphoreType.DMA((5,)),
            pltpu.SemaphoreType.DMA((5, 3)),
            pltpu.SemaphoreType.DMA((5,)),
            pltpu.SemaphoreType.DMA((PASSES,)),
            pltpu.SemaphoreType.DMA((PASSES,)),
            pltpu.SemaphoreType.DMA((PASSES,)),
            pltpu.SemaphoreType.DMA((PASSES,)),
            pltpu.SemaphoreType.DMA((PASSES,)),
            pltpu.SemaphoreType.DMA((PASSES,)),
            pltpu.SemaphoreType.DMA((PASSES,)),
        ],
        compiler_params=pltpu.CompilerParams(
            collective_id=0, has_side_effects=True, vmem_limit_bytes=48 * 1024 * 1024
        ),
    )(hist_lesser, hist_retarded, propagator, coupling, mf_weight, lag_weight, table)


def solution(mesh):
    table = momentum_table()

    def step(*args):
        return jax.shard_map(
            on_device,
            mesh=mesh,
            in_specs=(
                P(None, None, None),
                P(None, "mom", None, "tm"),
                P(None, "mom", None, "tm"),
                P(None, "mom", None, None),
                P(),
                P(),
                P(),
            ),
            out_specs=P(None, "mom", None, "tm"),
            check_vma=False,
        )(jnp.asarray(table), *args)

    return step
```

time: 1260 us -> 66.4 us (0.05); the launches traced: 1240 us -> 66.1 us
  blocking collectives: 739 us -> 0 us
  waiting for transfers between devices: 206 us -> 0 us
  matrix products: 101 us -> 0 us
  local copies, waits for them, and re-layouts: 92.5 us -> 6.5 us
  starting transfers between devices: 65.9 us -> 0 us
  Pallas kernels: 0 us -> 59.6 us
  other arithmetic: 25.2 us -> 0 us
  between operations: 14.7 us -> 0.02 us
    psum x3 -> x0, blocking collectives: 739 us -> none  [self_energies(): occupation = lax.psum(own_total, 'mom') / (KX * KY)]
    psum x3 -> x0, waiting for transfers between devices: 130 us -> none  [broadcast(): return lax.psum(jnp.where(mine, x, jnp.zeros_like(x)), axis)]
    dot_general x64 -> x0, matrix products: 101 us -> none  [the longest x7 11.5 us: complex_product(): jnp.einsum(pattern, first[0], second[0], precision=HIGHEST)]
    all_to_all x9 -> x0, waiting for transfers between devices: 76.5 us -> none  [the longest x3 30.2 us: self_energies(): lax.all_to_all(outgoing, 'mom', split_axis=2, concat_axis=1, tiled=True)]
    pallas_call x0 -> x1, Pallas kernels: none -> 59.6 us  [on_device(): pl.pallas_call(kernel, out_shape=jax.ShapeDtypeStruct(hist_lesser.shape,...]
    all_to_all x9 -> x0, starting transfers between devices: 58.1 us -> none  [the longest x3 31.3 us: self_energies(): lax.all_to_all(outgoing, 'mom', split_axis=2, concat_axis=1, tiled=True)]
    reshape x21 -> x0, local copies, waits for them, and re-layouts: 34.6 us -> none  [the longest x3 15.9 us: self_energies(): outgoing = window.reshape(2, momenta_here, ORB * ORB * W)]
    unnamed x55 -> x15, local copies, waits for them, and re-layouts: 35 us -> 6.5 us
  transfers between devices with their start and end apart: 14 -> 0, of which waited for: 12 -> 0; matrix products, arithmetic and copies ran while one was open for 2% -> 0% of each run, Pallas kernels for 0% -> 0%
where the time goes in v1:
time: 66.4 us; the launch traced here: 66.1 us
  Pallas kernels  59.6 us (90%)
  local copies, waits for them, and re-layouts  6.5 us (10%)
    pallas_call x1, Pallas kernels, on_device(): pl.pallas_call(kernel, out_shape=jax.ShapeDtypeStruct(hist_lesser.shape,...  59.6 us
    unnamed x15, local copies, waits for them, and re-layouts  6.5 us

profile of v1, /device:TPU:1, one launch (start us, length us, event | category | flops | bytes accessed | tf_op | source)
XLA Modules:
  0.0 66.1 jit_solution(17784202364138914421)
XLA Ops:
  0.0 0.0 copy-start
  0.0 1.0 %copy-done = bf16[2,256,512]{2,1,0:T(8,128)(2,1)S(1)} copy-done((bf16[2,256,512]{2,1,0:T(8,128)(2,1)S(1)}, bf16[2,256,512]{2,1,0:T(8,128)(2,1)}, u32[]{:S(2)}) %copy-start) | copy-done | bytes 524312
  1.0 0.0 copy-start.1
  1.0 0.9 %copy-done.1 = f32[2,4,16,512]{3,2,1,0:T(8,128)S(1)} copy-done((f32[2,4,16,512]{3,2,1,0:T(8,128)S(1)}, f32[2,4,16,512]{3,2,1,0:T(8,128)}, u32[]{:S(2)}) %copy-start.1) | copy-done | bytes 262168
  2.0 0.0 copy-start.2
  2.0 0.9 %copy-done.2 = f32[2,4,16,512]{3,2,1,0:T(8,128)S(1)} copy-done((f32[2,4,16,512]{3,2,1,0:T(8,128)S(1)}, f32[2,4,16,512]{3,2,1,0:T(8,128)}, u32[]{:S(2)}) %copy-start.2) | copy-done | bytes 262168
  2.9 0.0 copy-start.3
  2.9 0.8 %copy-done.3 = f32[2,4,16,16]{3,2,1,0:T(8,128)S(1)} copy-done((f32[2,4,16,16]{3,2,1,0:T(8,128)S(1)}, f32[2,4,16,16]{3,2,1,0:T(8,128)}, u32[]{:S(2)}) %copy-start.3) | copy-done | bytes 8216
  3.8 0.0 copy-start.4
  3.8 0.7 %copy-done.4 = f32[256]{0:T(256)S(1)} copy-done((f32[256]{0:T(256)S(1)}, f32[256]{0:T(256)}, u32[]{:S(2)}) %copy-start.4) | copy-done | bytes 1048
  4.5 0.0 copy-start.5
  4.5 0.7 %copy-done.5 = f32[256]{0:T(256)S(1)} copy-done((f32[256]{0:T(256)S(1)}, f32[256]{0:T(256)}, u32[]{:S(2)}) %copy-start.5) | copy-done | bytes 1048
  5.1 0.0 copy-start.6
  5.1 0.7 copy-done.6
  5.8 59.6 %shard_map.73 = f32[2,4,16,512]{3,2,1,0:T(8,128)S(1)} custom-call(f32[2,4,16,512]{3,2,1,0:T(8,128)S(1)} %copy-done.1, f32[2,4,16,512]{3,2,1,0:T(8,128)S(1)} %copy-done.2, f32[2,4,16,16]{3,2,1,0:T(8,128)S(1)} %copy-done.3, f32[256]{0:T(256)S(1)} %copy-done.4, f32[256]{0:T(256)S(1)} %copy-done.5, f32[8]{0:T(128)S(1)} %copy-done.6, bf16[2,256,512]{2,1,0:T(8,128)(2,1)S(1)} %copy-done), custom_call_target="tpu_custom_call" | custom-call | tf_op jit(solution)/shard_map/pallas_call | solution.py:365
  65.4 0.7 %copy.9 = f32[2,4,16,512]{3,2,1,0:T(8,128)} copy(f32[2,4,16,512]{3,2,1,0:T(8,128)S(1)} %shard_map.73) | data formatting | bytes 524288
Async XLA Ops:
  0.0 1.0 %copy-start = (bf16[2,256,512]{2,1,0:T(8,128)(2,1)S(1)}, bf16[2,256,512]{2,1,0:T(8,128)(2,1)}, u32[]{:S(2)}) copy-start(bf16[2,256,512]{2,1,0:T(8,128)(2,1)} %constant.2.clone.table) | copy-start | bytes 1572868
  1.0 0.9 %copy-start.1 = (f32[2,4,16,512]{3,2,1,0:T(8,128)S(1)}, f32[2,4,16,512]{3,2,1,0:T(8,128)}, u32[]{:S(2)}) copy-start(f32[2,4,16,512]{3,2,1,0:T(8,128)} %hl.1) | copy-start | bytes 786436
  2.0 0.9 %copy-start.2 = (f32[2,4,16,512]{3,2,1,0:T(8,128)S(1)}, f32[2,4,16,512]{3,2,1,0:T(8,128)}, u32[]{:S(2)}) copy-start(f32[2,4,16,512]{3,2,1,0:T(8,128)} %hr.1) | copy-start | bytes 786436
  2.9 0.8 %copy-start.3 = (f32[2,4,16,16]{3,2,1,0:T(8,128)S(1)}, f32[2,4,16,16]{3,2,1,0:T(8,128)}, u32[]{:S(2)}) copy-start(f32[2,4,16,16]{3,2,1,0:T(8,128)} %prop.1) | copy-start | bytes 24580
  3.8 0.7 %copy-start.4 = (f32[256]{0:T(256)S(1)}, f32[256]{0:T(256)}, u32[]{:S(2)}) copy-start(f32[256]{0:T(256)} %coup.1) | copy-start | bytes 3076
  4.5 0.7 %copy-start.5 = (f32[256]{0:T(256)S(1)}, f32[256]{0:T(256)}, u32[]{:S(2)}) copy-start(f32[256]{0:T(256)} %mf.1) | copy-start | bytes 3076
  5.1 0.7 copy-start.6

commit v2 on v1

--- a/solution.py
+++ b/solution.py
@@ -52,9 +52,9 @@
 
 
 def kernel(
-    hl, hr, prop, coup, mf, lag, table,
+    hl, hr, prop_hbm, coup_hbm, mf_hbm, lag_hbm, table,
     out,
-    hlv, hrv, wl, wr, tab, startv, startw, hank, sendf, fbuf, sendb, rbuf,
+    prop, coup, mf, lag, hlv, hrv, wl, wr, tab, startv, startw, hank, sendf, fbuf, sendb, rbuf,
     load_sem, x_send, x_recv, f_send, f_recv, f_own, s_send, s_recv, b_send, b_recv,
 ):
     dev = lax.axis_index("mom")
@@ -85,6 +85,14 @@
         barrier, inc=1, device_id={"mom": chip * 2 + 1 - core, "tm": x}, device_id_type=MESH
     )
 
+    small = [
+        pltpu.make_async_copy(source, place, load_sem.at[5 + slot])
+        for slot, (source, place) in enumerate(
+            ((prop_hbm, prop), (coup_hbm, coup), (mf_hbm, mf), (lag_hbm, lag))
+        )
+    ]
+    for load in small:
+        load.start()
     loads = [
         pltpu.make_async_copy(hl, hlv.at[:, :, :, pl.ds(LANES, BLOCKS * LANES)], load_sem.at[0]),
         pltpu.make_async_copy(hr, hrv.at[:, :, :, pl.ds(LANES, BLOCKS * LANES)], load_sem.at[1]),
@@ -142,6 +150,8 @@
         hlv[:, :, :, pl.ds(0, LANES)] = zeros
         hrv[:, :, :, pl.ds(0, LANES)] = zeros
 
+    for load in small:
+        load.wait()
     lane = lax.broadcasted_iota(jnp.int32, (1, LANES), 1)
     low_half = lane < HALF
     sign = jnp.where(low_half, -1.0, 1.0).astype(F32)
@@ -359,15 +369,18 @@
 
 def on_device(table, hist_lesser, hist_retarded, propagator, coupling, mf_weight, lag_weight):
     vmem = pl.BlockSpec(memory_space=pltpu.VMEM)
-    smem = pl.BlockSpec(memory_space=pltpu.SMEM)
-    anywhere = pl.BlockSpec(memory_space=pl.ANY)
+    hbm = pl.BlockSpec(memory_space=pltpu.HBM)
     padded = (2, HERE, ORB, (BLOCKS + 1) * LANES)
     return pl.pallas_call(
         kernel,
         out_shape=jax.ShapeDtypeStruct(hist_lesser.shape, F32),
-        in_specs=[anywhere, anywhere, vmem, smem, smem, smem, anywhere],
+        in_specs=[hbm] * 7,
         out_specs=vmem,
         scratch_shapes=[
+            pltpu.VMEM((2, HERE, ORB, ORB), F32),
+            pltpu.SMEM((ORB * ORB,), F32),
+            pltpu.SMEM((ORB * ORB,), F32),
+            pltpu.SMEM((W,), F32),
             pltpu.VMEM(padded, F32),
             pltpu.VMEM(padded, F32),
             pltpu.VMEM((2, HERE, ORB, 2 * LANES), F32),
@@ -380,7 +393,7 @@
             pltpu.VMEM((PASSES, KX * KY, LANES), F32),
             pltpu.VMEM((PASSES, CHIPS, 8, LANES), F32),
             pltpu.VMEM((PASSES, 2, ORB * 8, LANES), F32),
-            pltpu.SemaphoreType.DMA((5,)),
+            pltpu.SemaphoreType.DMA((9,)),
             pltpu.SemaphoreType.DMA((5, 3)),
             pltpu.SemaphoreType.DMA((5,)),
             pltpu.SemaphoreType.DMA((PASSES,)),
@@ -392,7 +405,7 @@
             pltpu.SemaphoreType.DMA((PASSES,)),
         ],
         compiler_params=pltpu.CompilerParams(
-            collective_id=0, has_side_effects=True, vmem_limit_bytes=48 * 1024 * 1024
+            collective_id=0, has_side_effects=True, vmem_limit_bytes=67043328
         ),
     )(hist_lesser, hist_retarded, propagator, coupling, mf_weight, lag_weight, table)
 

time: 66.4 us -> 61.9 us (0.932)
  local copies, waits for them, and re-layouts: 6.5 us -> 1.67 us
    unnamed x15 -> x1, local copies, waits for them, and re-layouts: 6.5 us -> 1.67 us
where the time goes in v2:
time: 61.9 us; the launch traced here: 61.5 us
  Pallas kernels  59.8 us (97%)
  local copies, waits for them, and re-layouts  1.67 us (3%)
    pallas_call x1, Pallas kernels, on_device(): pl.pallas_call(kernel, out_shape=jax.ShapeDtypeStruct(hist_lesser.shape,...  59.8 us
    unnamed x1, local copies, waits for them, and re-layouts  1.67 us

profile of v2, /device:TPU:1, one launch (start us, length us, event | category | flops | bytes accessed | tf_op | source)
XLA Modules:
  0.0 61.5 jit_solution(5887932100925852253)
XLA Ops:
  0.0 59.8 %shard_map.73 = f32[2,4,16,512]{3,2,1,0:T(8,128)} custom-call(f32[2,4,16,512]{3,2,1,0:T(8,128)} %hl.1, f32[2,4,16,512]{3,2,1,0:T(8,128)} %hr.1, f32[2,4,16,16]{3,2,1,0:T(8,128)} %prop_hbm.1, f32[256]{0:T(256)} %coup_hbm.1, f32[256]{0:T(256)} %mf_hbm.1, f32[8]{0:T(128)} %lag_hbm.1, bf16[2,256,512]{2,1,0:T(8,128)(2,1)} %constant.2.clone.table), custom_call_target="tpu_custom_call" | custom-call | tf_op jit(solution)/shard_map/pallas_call | solution.py:374
  59.8 1.7 %copy.9 = f32[2,4,16,512]{3,2,1,0:T(8,128)} copy(f32[2,4,16,512]{3,2,1,0:T(8,128)} %shard_map.73) | data formatting | bytes 524288

commit v3 on v0

v3 whole, which is shorter than its diff:
```python
import math

import jax
import jax.numpy as jnp
import ml_dtypes
import numpy as np
from jax import lax
from jax.experimental import pallas as pl
from jax.experimental.pallas import tpu as pltpu
from jax.sharding import PartitionSpec as P

KX = 16
KY = 16
K = KX * KY
ORB = 16
W = 8
PASSES = 3
NZ, NY = 8, 4
CHIPS = NZ * NY
CORES = 2
TM = 4
HERE = 4
LANES = W * ORB
QUARTER = LANES // 4
HALF = LANES // 2
BLOCKS = 4

MESH = pl.DeviceIdType.MESH
F32 = jnp.float32
BF16 = jnp.bfloat16


def halves(full):
    full = full.astype(np.float32)
    high = full.astype(ml_dtypes.bfloat16)
    low = (full - high.astype(np.float32)).astype(ml_dtypes.bfloat16)
    return np.stack([high, low])


def momentum_tables():
    place = np.arange(K)

    def number(core, chip, here):
        return 8 * chip + 4 * core + here

    plain = number(place // 128, place // 4 % 32, place % 4)
    parted = number(place // 64 % 2, place // 2 % 32, place % 2 + 2 * (place // 128))

    def table(rows, columns):
        turn = (rows[:, None] // KY) * (columns[None, :] // KY) % KX
        turn = turn + (rows[:, None] % KY) * (columns[None, :] % KY) % KY
        phase = 2.0 * math.pi * turn / 16.0
        return halves(np.concatenate([np.cos(phase), np.sin(phase)], axis=1) / 16.0)

    return np.stack([table(plain, parted), table(plain, plain)])


def split(x):
    high = x.astype(BF16)
    return high, (x - high.astype(F32)).astype(BF16)


def mm(a, b):
    return jnp.dot(a, b, preferred_element_type=F32)


def ring(step, size):
    return min(step % size, -step % size)


def offsets(limit):
    found = [(dz, dy) for dz in range(NZ) for dy in range(NY) if ring(dz, NZ) + ring(dy, NY) <= limit]
    return sorted(found, key=lambda o: -(ring(o[0], NZ) + ring(o[1], NY)))


def kernel(
    hl, hr, prop_hbm, coup_hbm, mf_hbm, lag_hbm, tables,
    out,
    prop, propw, coup, mf, lag, hlv, hrv, wl, wr, tabs, startv, startw, hank, sendf, fbuf, sendb, rbuf,
    load_sem, x_send, x_recv, f_send, f_recv, f_own, b_send, b_recv,
):
    dev = lax.axis_index("mom")
    x = lax.axis_index("tm")
    core = lax.rem(dev, CORES)
    chip = dev // CORES
    z = chip // NY
    y = lax.rem(chip, NY)
    mate = x + 1 - 2 * lax.rem(x, 2)
    odd = lax.rem(x, 2)

    def place(dz, dy):
        return lax.rem(z + dz, NZ), lax.rem(y + dy, NY)

    def label_of(zz, yy, plane_odd):
        shift = 1 - plane_odd
        return lax.rem(zz + (NZ // 2) * shift, NZ) * NY + lax.rem(yy + (NY // 2) * shift, NY)

    def device(zz, yy, cc, plane):
        return {"mom": (zz * NY + yy) * CORES + cc, "tm": plane}

    def each(limit, plane, plane_odd, own):
        for dz, dy in offsets(limit):
            zz, yy = place(dz, dy)
            for flip in (1, 0):
                if own and not (dz or dy or flip):
                    continue
                cc = 1 - core if flip else core
                yield zz, yy, cc, plane, plane_odd

    label = label_of(z, y, odd)
    row = label // 2
    quarter = lax.rem(label, 2) * 2 + core
    slot_here = core * CHIPS + label
    far = NZ + NY

    def near(limit_own, limit_mate):
        yield from each(limit_mate, mate, 1 - odd, False)
        yield from each(limit_own, x, odd, True)

    barrier = pltpu.get_barrier_semaphore()

    def greet(targets):
        for zz, yy, cc, plane, _ in targets:
            pl.semaphore_signal(barrier, inc=1, device_id=device(zz, yy, cc, plane), device_id_type=MESH)

    @pl.when(x == 3)
    def _():
        greet(near(far, 2))

    @pl.when(x == 2)
    def _():
        greet(near(3, far))
        greet([(z, y, core, 1, 1)])

    @pl.when(x < 2)
    def _():
        greet(each(3, 3 - x, 1 - odd, False))
        greet(each(2, 2 + x, odd, False))
        greet(near(3, 2))

    small = [
        pltpu.make_async_copy(source, target, load_sem.at[4 + number])
        for number, (source, target) in enumerate(
            ((prop_hbm, prop), (coup_hbm, coup), (mf_hbm, mf), (lag_hbm, lag))
        )
    ]
    own_window = [
        pltpu.make_async_copy(hl.at[:, :, :, pl.ds(2 * LANES, 2 * LANES)], wl, load_sem.at[8]),
        pltpu.make_async_copy(hr.at[:, :, :, pl.ds(2 * LANES, 2 * LANES)], wr, load_sem.at[9]),
        pltpu.make_async_copy(prop_hbm, propw, load_sem.at[10]),
    ]
    loads = [
        pltpu.make_async_copy(hl, hlv.at[:, :, :, pl.ds(LANES, BLOCKS * LANES)], load_sem.at[0]),
        pltpu.make_async_copy(hr, hrv.at[:, :, :, pl.ds(LANES, BLOCKS * LANES)], load_sem.at[1]),
    ]
    tables_in = pltpu.make_async_copy(tables, tabs, load_sem.at[2])

    @pl.when(x == 3)
    def _():
        for copy in own_window:
            copy.start()

    for load in small + loads:
        load.start()
    tables_in.start()
    for load in small:
        load.wait()

    lane = lax.broadcasted_iota(jnp.int32, (1, LANES), 1)
    low_half = lane < HALF
    block_of_lane = lane // QUARTER
    first_of_two = lax.rem(block_of_lane, 2) == 0
    sign = jnp.where(first_of_two, -1.0, 1.0).astype(F32)

    coup_lane = jnp.zeros((1, LANES), F32)
    mf_lane = jnp.zeros((1, LANES), F32)
    for b in range(ORB):
        here = lax.rem(lane, ORB) == b
        coup_lane = jnp.where(here, coup[row * ORB + b], coup_lane)
        mf_lane = jnp.where(here, mf[row * ORB + b], mf_lane)
    strength = coup_lane * coup_lane
    newest = (lax.rem(lane, QUARTER) >= QUARTER - ORB) & (quarter == 3)
    mf_lane = jnp.where(newest, mf_lane, 0.0)
    first_row = lax.broadcasted_iota(jnp.int32, (K, 1), 0) == 0
    mf_term = jnp.where(first_row, mf_lane, 0.0)

    def turn(value):
        return jnp.where(
            first_of_two, pltpu.roll(value, LANES - QUARTER, 1), pltpu.roll(value, QUARTER, 1)
        )

    def transpose_blocks(parts):
        result = []
        for j in range(4):
            total = parts[j]
            for i in range(4):
                if i == j:
                    continue
                moved = pltpu.roll(parts[i], (QUARTER * (i - j)) % LANES, 1)
                total = jnp.where(block_of_lane == i, moved, total)
            result.append(total)
        return result

    def propagate(step, k, source, lanes_from, count):
        stack = jnp.concatenate([step[0, k], step[1, k]], axis=0)
        real, imag = (
            jnp.dot(
                stack, source[c, k, :, pl.ds(lanes_from, count)],
                precision=lax.Precision.HIGHEST, preferred_element_type=F32,
            )
            for c in range(2)
        )
        return real[:ORB] - imag[ORB:], real[ORB:] + imag[:ORB]

    def build(k, slot, source_r, source_l, lanes_from):
        for lp, source in enumerate((source_r, source_l)):
            for c in range(2):
                first = source[c, k, :, pl.ds(lanes_from, LANES)]
                second = source[c, k, :, pl.ds(lanes_from + LANES, LANES)]
                for m in range(W):
                    shift = ORB * (m + 1)
                    if shift < LANES:
                        moved = pltpu.roll(jnp.where(lane >= shift, first, second), LANES - shift, 1)
                    else:
                        moved = second
                    high, low = split(moved * lag[m])
                    at = lp * LANES + m * ORB
                    hank[slot, 0, pl.ds(at, ORB), pl.ds(c * LANES, LANES)] = high
                    hank[slot, 1, pl.ds(at, ORB), pl.ds(c * LANES, LANES)] = low

    def build_blocks(blocks):
        @pl.loop(0, HERE)
        def _(k):
            for block in blocks:
                build(k, block * HERE + k, hrv, hlv, block * LANES)

    def pack_window(p, reals, imags):
        for r in range(2):
            parts = transpose_blocks([reals[r], imags[r], reals[r + 2], imags[r + 2]])
            for w in range(4):
                sendf[p, w, pl.ds(r, ORB, stride=2), :] = parts[w]

    def forward_copy(p, target):
        zz, yy, cc, plane, plane_odd = target
        goal = label_of(zz, yy, plane_odd)
        return pltpu.make_async_remote_copy(
            src_ref=sendf.at[p, lax.rem(goal, 2) * 2 + cc, pl.ds((goal // 2) * 2, 2), :],
            dst_ref=fbuf.at[p, pl.ds(slot_here * 2, 2), :],
            send_sem=f_send.at[p], recv_sem=f_recv.at[p],
            device_id=device(zz, yy, cc, plane), device_id_type=MESH,
        )

    def own_forward(p):
        return pltpu.make_async_copy(
            sendf.at[p, quarter, pl.ds(row * 2, 2), :],
            fbuf.at[p, pl.ds(slot_here * 2, 2), :],
            f_own.at[p],
        )

    def goal_slot(p, zz, yy, cc, plane_odd):
        goal = label_of(zz, yy, plane_odd) if p < PASSES - 1 else zz * NY + yy
        return cc * CHIPS + goal

    def back_copy(p, target):
        zz, yy, cc, plane, plane_odd = target
        return pltpu.make_async_remote_copy(
            src_ref=sendb.at[p, pl.ds(goal_slot(p, zz, yy, cc, plane_odd) * HERE, HERE), :],
            dst_ref=rbuf.at[p, quarter, pl.ds(row * HERE, HERE), :],
            send_sem=b_send.at[p], recv_sem=b_recv.at[p],
            device_id=device(zz, yy, cc, plane), device_id_type=MESH,
        )

    def own_back(p):
        return pltpu.make_async_copy(
            sendb.at[p, pl.ds(goal_slot(p, z, y, core, odd) * HERE, HERE), :],
            rbuf.at[p, quarter, pl.ds(row * HERE, HERE), :],
            f_own.at[PASSES + p],
        )

    def wait_rows(rows, sem):
        some = sendb.at[0, pl.ds(0, rows), :]
        pltpu.make_async_copy(some, some, sem).wait()

    others = CHIPS * CORES - 1

    def real_space(p):
        here = fbuf[p]
        both = jnp.concatenate([here, turn(here) * sign], axis=0)
        high = both.astype(BF16).astype(F32)
        low = both - high
        front = jnp.where(low_half, high, pltpu.roll(low, HALF, 1)).astype(BF16)
        rear = jnp.where(low_half, pltpu.roll(high, HALF, 1), low).astype(BF16)
        count = K // 2
        stack = jnp.concatenate([front[:count], rear[:count], front[count:], rear[count:]], axis=0)
        main = mm(tabs[0, 0], stack)
        rest = mm(tabs[0, 1], stack)
        pos = main + pltpu.roll(main, HALF, 1) + jnp.where(low_half, rest, pltpu.roll(rest, HALF, 1))
        turned = turn(pos)
        square = pos * pos
        turned_square = turned * turned
        lesser = (strength * (square + turned_square) + mf_term) * pos
        pair = strength * jnp.where(first_of_two, square - turned_square, 2.0 * pos * turned)
        both = jnp.where(low_half, lesser, pair)
        high, low = split(jnp.concatenate([both, turn(both) * -sign], axis=0))
        main = mm(tabs[1, 0], jnp.concatenate([high, low], axis=1))
        sendb[p] = main[:, :LANES] + main[:, LANES:] + mm(tabs[1, 1], high)

    def send_back(p):
        own_back(p).start()
        for target in near(3, 2):
            back_copy(p, target).start()

    def wait_back(p):
        own_back(p).wait()
        wait_rows(others * HERE, b_recv.at[p])

    def arrived(p, k):
        parts = transpose_blocks([rbuf[p, w, pl.ds(k, ORB, stride=HERE), :] for w in range(4)])
        lesser_real, lesser_imag, pair_real, pair_imag = parts
        high, low = split(
            jnp.concatenate(
                [
                    jnp.concatenate([lesser_real, pair_real], axis=1),
                    jnp.concatenate([lesser_imag, pair_imag], axis=1),
                ],
                axis=0,
            )
        )
        return jnp.concatenate([high, low], axis=0)

    def collide(stack, slot):
        rows = 2 * ORB
        product = mm(stack, hank[slot, 0])
        total = product[:rows] + product[rows:] + mm(stack[:rows], hank[slot, 1])
        real = total[:ORB, :LANES] - total[ORB:, LANES:]
        imag = total[:ORB, LANES:] + total[ORB:, :LANES]
        return real, imag

    def start_window():
        reals, imags = [], []
        for k in range(HERE):
            real, imag = propagate(propw, k, wl, LANES, LANES)
            startw[0, k] = real
            startw[1, k] = imag
            reals.append(real)
            imags.append(imag)
        return reals, imags

    def window_copy(part):
        src, dst = ((hr.at[:, :, :, pl.ds(2 * LANES, 2 * LANES)], wr),
                    (hl.at[:, :, :, pl.ds(2 * LANES, 2 * LANES)], wl),
                    (prop_hbm, propw))[part]
        zz, yy = place(NZ // 2, NY // 2)
        return pltpu.make_async_remote_copy(
            src_ref=src, dst_ref=dst, send_sem=x_send.at[part], recv_sem=x_recv.at[part],
            device_id=device(zz, yy, core, 2), device_id_type=MESH,
        )

    def rim_copy(part):
        src, dst = ((hl, hlv), (hr, hrv))[part]
        return pltpu.make_async_remote_copy(
            src_ref=src.at[:, :, :, pl.ds((BLOCKS - 1) * LANES, LANES)],
            dst_ref=dst.at[:, :, :, pl.ds(0, LANES)],
            send_sem=x_send.at[3 + part], recv_sem=x_recv.at[3 + part],
            device_id=device(z, y, core, lax.rem(x + 1, TM)), device_id_type=MESH,
        )

    @pl.when(x == 3)
    def _():
        for copy in own_window:
            copy.wait()
        pack_window(0, *start_window())
        own_forward(0).start()
        pl.semaphore_wait(barrier, others + 2 * (others + 1))
        for target in each(far, 2, 0, False):
            forward_copy(0, target).start()
        for target in each(far, 3, 1, True):
            forward_copy(0, target).start()
        for part in range(3):
            window_copy(part).start()

    @pl.when(x == 2)
    def _():
        pl.semaphore_wait(barrier, others + others + 1)

    @pl.when(x == 1)
    def _():
        pl.semaphore_wait(barrier, others + 1)

    @pl.when(x == 0)
    def _():
        pl.semaphore_wait(barrier, others)

    @pl.when(x < TM - 1)
    def _():
        for part in range(2):
            rim_copy(part).start()

    @pl.when(x == 0)
    def _():
        zeros = jnp.zeros((2, HERE, ORB, LANES), F32)
        hlv[:, :, :, pl.ds(0, LANES)] = zeros
        hrv[:, :, :, pl.ds(0, LANES)] = zeros

    for load in loads:
        load.wait()

    def start_all():
        @pl.loop(0, HERE)
        def _(k):
            real, imag = propagate(prop, k, hlv, LANES, BLOCKS * LANES)
            startv[0, k] = real
            startv[1, k] = imag

    start_all()
    build_blocks((1, 2, 3))
    tables_in.wait()

    @pl.when(x >= 2)
    def _():
        for p in range(PASSES - 1):
            if p == 0:
                @pl.when(x == 3)
                def _():
                    own_forward(0).wait()
                    wait_rows(others * 2, f_recv.at[0])

                @pl.when(x == 2)
                def _():
                    wait_rows((others + 1) * 2, f_recv.at[0])
            else:
                own_forward(p).wait()
                wait_rows(others * 2, f_recv.at[p])
            real_space(p)
            send_back(p)
            if p == 0:
                @pl.when(x == 2)
                def _():
                    for part in range(3):
                        window_copy(part).wait_recv()
                    start_window()

                @pl.loop(0, HERE)
                def _(k):
                    build(k, BLOCKS * HERE + k, wr, wl, 0)

            wait_back(p)
            reals, imags = [], []
            for k in range(HERE):
                real, imag = collide(arrived(p, k), BLOCKS * HERE + k)
                reals.append(startw[0, k] + imag)
                imags.append(startw[1, k] - real)
            pack_window(p + 1, reals, imags)
            own_forward(p + 1).start()
            if p + 1 == PASSES - 1:
                for target in each(3, 3 - x, 1 - odd, False):
                    forward_copy(p + 1, target).start()
                for target in each(2, x - 2, odd, False):
                    forward_copy(p + 1, target).start()
            for target in near(3, 2):
                forward_copy(p + 1, target).start()

    @pl.when(x > 0)
    def _():
        for part in range(2):
            rim_copy(part).wait_recv()

    build_blocks((0,))

    p = PASSES - 1

    @pl.when(x >= 2)
    def _():
        own_forward(p).wait()
        wait_rows(others * 2, f_recv.at[p])

    @pl.when(x < 2)
    def _():
        wait_rows((others + 1) * 2, f_recv.at[p])

    real_space(p)
    send_back(p)
    wait_back(p)
    for k in range(HERE):
        stack = arrived(p, k)
        for block in range(BLOCKS):
            real, imag = collide(stack, block * HERE + k)
            at = pl.ds(block * LANES, LANES)
            out[0, k, :, at] = startv[0, k, :, at] + imag
            out[1, k, :, at] = startv[1, k, :, at] - real

    wait_rows(others * HERE, b_send.at[p])

    @pl.when(x >= 2)
    def _():
        wait_rows(others * HERE, b_send.at[0])
        wait_rows(others * HERE, b_send.at[1])
        wait_rows(others * 2, f_send.at[1])
        wait_rows((2 * others + 1) * 2, f_send.at[2])

    @pl.when(x == 3)
    def _():
        wait_rows((2 * others + 1) * 2, f_send.at[0])
        for part in range(3):
            window_copy(part).wait_send()

    @pl.when(x < TM - 1)
    def _():
        for part in range(2):
            rim_copy(part).wait_send()


def on_device(tables, hist_lesser, hist_retarded, propagator, coupling, mf_weight, lag_weight):
    vmem = pl.BlockSpec(memory_space=pltpu.VMEM)
    hbm = pl.BlockSpec(memory_space=pltpu.HBM)
    padded = (2, HERE, ORB, (BLOCKS + 1) * LANES)
    return pl.pallas_call(
        kernel,
        out_shape=jax.ShapeDtypeStruct(hist_lesser.shape, F32),
        in_specs=[hbm] * 7,
        out_specs=vmem,
        scratch_shapes=[
            pltpu.VMEM((2, HERE, ORB, ORB), F32),
            pltpu.VMEM((2, HERE, ORB, ORB), F32),
            pltpu.SMEM((ORB * ORB,), F32),
            pltpu.SMEM((ORB * ORB,), F32),
            pltpu.SMEM((W,), F32),
            pltpu.VMEM(padded, F32),
            pltpu.VMEM(padded, F32),
            pltpu.VMEM((2, HERE, ORB, 2 * LANES), F32),
            pltpu.VMEM((2, HERE, ORB, 2 * LANES), F32),
            pltpu.VMEM((2, 2, K, 2 * K), BF16),
            pltpu.VMEM((2, HERE, ORB, BLOCKS * LANES), F32),
            pltpu.VMEM((2, HERE, ORB, LANES), F32),
            pltpu.VMEM(((BLOCKS + 1) * HERE, 2, 2 * LANES, 2 * LANES), BF16),
            pltpu.VMEM((PASSES, 4, 2 * ORB, LANES), F32),
            pltpu.VMEM((PASSES, K // 2, LANES), F32),
            pltpu.VMEM((PASSES, K, LANES), F32),
            pltpu.VMEM((PASSES, 4, HERE * ORB, LANES), F32),
            pltpu.SemaphoreType.DMA((11,)),
            pltpu.SemaphoreType.DMA((5,)),
            pltpu.SemaphoreType.DMA((5,)),
            pltpu.SemaphoreType.DMA((PASSES,)),
            pltpu.SemaphoreType.DMA((PASSES,)),
            pltpu.SemaphoreType.DMA((2 * PASSES,)),
            pltpu.SemaphoreType.DMA((PASSES,)),
            pltpu.SemaphoreType.DMA((PASSES,)),
        ],
        compiler_params=pltpu.CompilerParams(
            collective_id=0, has_side_effects=True, vmem_limit_bytes=67043328
        ),
    )(hist_lesser, hist_retarded, propagator, coupling, mf_weight, lag_weight, tables)


def solution(mesh):
    tables = momentum_tables()

    def step(*args):
        return jax.shard_map(
            on_device,
            mesh=mesh,
            in_specs=(
                P(None, None, None, None),
                P(None, "mom", None, "tm"),
                P(None, "mom", None, "tm"),
                P(None, "mom", None, None),
                P(),
                P(),
                P(),
            ),
            out_specs=P(None, "mom", None, "tm"),
            check_vma=False,
        )(jnp.asarray(tables), *args)

    return step
```

time: 1260 us -> 62.8 us (0.05); the launches traced: 1240 us -> 62.7 us
  blocking collectives: 739 us -> 0 us
  waiting for transfers between devices: 206 us -> 0 us
  matrix products: 101 us -> 0 us
  local copies, waits for them, and re-layouts: 92.5 us -> 1.67 us
  starting transfers between devices: 65.9 us -> 0 us
  Pallas kernels: 0 us -> 61 us
  other arithmetic: 25.2 us -> 0 us
  between operations: 14.7 us -> 0.01 us
    psum x3 -> x0, blocking collectives: 739 us -> none  [self_energies(): occupation = lax.psum(own_total, 'mom') / (KX * KY)]
    psum x3 -> x0, waiting for transfers between devices: 130 us -> none  [broadcast(): return lax.psum(jnp.where(mine, x, jnp.zeros_like(x)), axis)]
    dot_general x64 -> x0, matrix products: 101 us -> none  [the longest x7 11.5 us: complex_product(): jnp.einsum(pattern, first[0], second[0], precision=HIGHEST)]
    all_to_all x9 -> x0, waiting for transfers between devices: 76.5 us -> none  [the longest x3 30.2 us: self_energies(): lax.all_to_all(outgoing, 'mom', split_axis=2, concat_axis=1, tiled=True)]
    pallas_call x0 -> x1, Pallas kernels: none -> 61 us  [on_device(): pl.pallas_call(kernel, out_shape=jax.ShapeDtypeStruct(hist_lesser.shape,...]
    all_to_all x9 -> x0, starting transfers between devices: 58.1 us -> none  [the longest x3 31.3 us: self_energies(): lax.all_to_all(outgoing, 'mom', split_axis=2, concat_axis=1, tiled=True)]
    reshape x21 -> x0, local copies, waits for them, and re-layouts: 34.6 us -> none  [the longest x3 15.9 us: self_energies(): outgoing = window.reshape(2, momenta_here, ORB * ORB * W)]
    unnamed x55 -> x1, local copies, waits for them, and re-layouts: 35 us -> 1.67 us
  transfers between devices with their start and end apart: 14 -> 0, of which waited for: 12 -> 0; matrix products, arithmetic and copies ran while one was open for 2% -> 0% of each run, Pallas kernels for 0% -> 0%
where the time goes in v3:
time: 62.8 us; the launch traced here: 62.7 us
  Pallas kernels  61 us (97%)
  local copies, waits for them, and re-layouts  1.67 us (3%)
    pallas_call x1, Pallas kernels, on_device(): pl.pallas_call(kernel, out_shape=jax.ShapeDtypeStruct(hist_lesser.shape,...  61 us
    unnamed x1, local copies, waits for them, and re-layouts  1.67 us

profile of v3, /device:TPU:1, one launch (start us, length us, event | category | flops | bytes accessed | tf_op | source)
XLA Modules:
  0.0 62.7 jit_solution(14606908062182790444)
XLA Ops:
  0.0 61.0 %shard_map.73 = f32[2,4,16,512]{3,2,1,0:T(8,128)} custom-call(f32[2,4,16,512]{3,2,1,0:T(8,128)} %hl.1, f32[2,4,16,512]{3,2,1,0:T(8,128)} %hr.1, f32[2,4,16,16]{3,2,1,0:T(8,128)} %prop_hbm.1, f32[256]{0:T(256)} %coup_hbm.1, f32[256]{0:T(256)} %mf_hbm.1, f32[8]{0:T(128)} %lag_hbm.1, bf16[2,2,256,512]{3,2,1,0:T(8,128)(2,1)} %constant.2.clone.tables), custom_call_target="tpu_custom_call" | custom-call | tf_op jit(solution)/shard_map/pallas_call | solution.py:517
  61.0 1.7 %copy.9 = f32[2,4,16,512]{3,2,1,0:T(8,128)} copy(f32[2,4,16,512]{3,2,1,0:T(8,128)} %shard_map.73) | data formatting | bytes 524288

commit v4 on v2

v4 whole, which is shorter than its diff:
```python
import math

import jax
import jax.numpy as jnp
import ml_dtypes
import numpy as np
from jax import lax
from jax.experimental import pallas as pl
from jax.experimental.pallas import tpu as pltpu
from jax.sharding import PartitionSpec as P

KX = 16
KY = 16
ORB = 16
W = 8
PASSES = 3
NZ, NY = 8, 4
CHIPS = NZ * NY
TM = 4
HERE = 4
LANES = W * ORB
HALF = LANES // 2
BLOCKS = 4

MESH = pl.DeviceIdType.MESH
F32 = jnp.float32
BF16 = jnp.bfloat16


def momentum_tables():
    place = np.arange(KX * KY)
    core, chip, here = place // 128, place // 4 % 32, place % 4
    k = 8 * chip + 4 * core + here
    kx, ky = k // KY, k % KY
    turn = (kx[:, None] * kx[None, :]) % KX + (ky[:, None] * ky[None, :]) % KY
    phase = 2.0 * math.pi * turn / 16.0
    full = np.stack([np.cos(phase), np.sin(phase)]).astype(np.float32) / 16.0
    high = full.astype(ml_dtypes.bfloat16)
    low = (full - high.astype(np.float32)).astype(ml_dtypes.bfloat16)
    both = np.stack([high, low])
    ahead = both.reshape(2, 2, 256, 2, 128).transpose(3, 0, 2, 1, 4).reshape(2, 2, 256, 256)
    back = both.reshape(2, 2, 2, 128, 256).transpose(2, 0, 3, 1, 4).reshape(2, 2, 128, 512)
    return ahead, back


def split(x):
    high = x.astype(BF16)
    return high, (x - high.astype(F32)).astype(BF16)


def mm(a, b):
    return jnp.dot(a, b, preferred_element_type=F32)


def ring(step, size):
    return min(step % size, -step % size)


OFFSETS = sorted(
    ((dz, dy) for dz in range(NZ) for dy in range(NY)), key=lambda o: -(ring(o[0], NZ) + ring(o[1], NY))
)


def kernel(
    hl, hr, prop_hbm, coup_hbm, mf_hbm, lag_hbm, ahead_hbm, back_hbm,
    out,
    prop, coup, mf, lag, hlv, hrv, ahead, backward, startv, hank, sendf, fbuf, sendb, rbuf,
    load_sem, x_send, x_recv, f_send, f_recv, f_own, s_send, s_recv, b_send, b_recv,
):
    dev = lax.axis_index("mom")
    x = lax.axis_index("tm")
    core = lax.rem(dev, 2)
    chip = dev // 2
    z = chip // NY
    y = lax.rem(chip, NY)
    row = chip // 2
    half = lax.rem(chip, 2)

    def peer_chip(dz, dy):
        return lax.rem(z + dz, NZ) * NY + lax.rem(y + dy, NY)

    others = CHIPS - 1
    last = TM - 1

    barrier = pltpu.get_barrier_semaphore()

    def greet(target, plane):
        pl.semaphore_signal(
            barrier, inc=1, device_id={"mom": target, "tm": plane}, device_id_type=MESH
        )

    @pl.when(x < last)
    def _():
        for dz, dy in OFFSETS:
            greet(peer_chip(dz, dy) * 2 + core, last)

    for dz, dy in OFFSETS[:-1]:
        greet(peer_chip(dz, dy) * 2 + core, x)
    greet(chip * 2 + 1 - core, x)

    @pl.when(x > 0)
    def _():
        greet(dev, x - 1)

    small = [
        pltpu.make_async_copy(source, place, load_sem.at[4 + slot])
        for slot, (source, place) in enumerate(
            ((prop_hbm, prop), (coup_hbm, coup), (mf_hbm, mf), (lag_hbm, lag))
        )
    ]
    for load in small:
        load.start()
    loads = [
        pltpu.make_async_copy(hl, hlv.at[:, :, :, pl.ds(LANES, BLOCKS * LANES)], load_sem.at[0]),
        pltpu.make_async_copy(hr, hrv.at[:, :, :, pl.ds(LANES, BLOCKS * LANES)], load_sem.at[1]),
        pltpu.make_async_copy(ahead_hbm, ahead, load_sem.at[2]),
        pltpu.make_async_copy(back_hbm.at[core], backward, load_sem.at[3]),
    ]
    for load in loads:
        load.start()

    def rim_copy(part):
        src, dst = ((hl, hlv), (hr, hrv))[part]
        return pltpu.make_async_remote_copy(
            src_ref=src.at[:, :, :, pl.ds(3 * LANES, LANES)],
            dst_ref=dst.at[:, :, :, pl.ds(0, LANES)],
            send_sem=x_send.at[part], recv_sem=x_recv.at[part],
            device_id={"mom": dev, "tm": lax.rem(x + 1, TM)}, device_id_type=MESH,
        )

    for load in small:
        load.wait()
    lane = lax.broadcasted_iota(jnp.int32, (1, LANES), 1)
    low_half = lane < HALF
    sign = jnp.where(low_half, -1.0, 1.0).astype(F32)

    coup_lane = jnp.zeros((1, LANES), F32)
    mf_lane = jnp.zeros((1, LANES), F32)
    for b in range(ORB):
        here = lax.rem(lane, ORB) == b
        coup_lane = jnp.where(here, coup[row * ORB + b], coup_lane)
        mf_lane = jnp.where(here, mf[row * ORB + b], mf_lane)
    strength = coup_lane * coup_lane
    newest = (lax.rem(lane, HALF) >= HALF - ORB) & (half == 1)
    mf_lane = jnp.where(newest, mf_lane, 0.0)
    first_row = lax.broadcasted_iota(jnp.int32, (KX * KY, 1), 0) == 0
    mf_term = jnp.where(first_row, mf_lane, 0.0)
    low_rows = lax.broadcasted_iota(jnp.int32, (1, 8, 1), 1) < 4

    def propagate(k, source, lanes_from, count):
        stack = jnp.concatenate([prop[0, k], prop[1, k]], axis=0)
        real = jnp.dot(
            stack, source[0, k, :, pl.ds(lanes_from, count)],
            precision=lax.Precision.HIGHEST, preferred_element_type=F32,
        )
        imag = jnp.dot(
            stack, source[1, k, :, pl.ds(lanes_from, count)],
            precision=lax.Precision.HIGHEST, preferred_element_type=F32,
        )
        return real[:ORB] - imag[ORB:], real[ORB:] + imag[:ORB]

    def build(k, slot, source_r, source_l, lanes_from):
        for lp, source in enumerate((source_r, source_l)):
            for c in range(2):
                first = source[c, k, :, pl.ds(lanes_from, LANES)]
                second = source[c, k, :, pl.ds(lanes_from + LANES, LANES)]
                for m in range(W):
                    shift = ORB * (m + 1)
                    if shift < LANES:
                        moved = pltpu.roll(
                            jnp.where(lane >= shift, first, second), LANES - shift, 1
                        )
                    else:
                        moved = second
                    high, low = split(moved * lag[m])
                    at = lp * LANES + m * ORB
                    hank[slot, 0, pl.ds(at, ORB), pl.ds(c * LANES, LANES)] = high
                    hank[slot, 1, pl.ds(at, ORB), pl.ds(c * LANES, LANES)] = low

    def send_window(p, k, real, imag):
        turned_real = pltpu.roll(real, HALF, 1)
        turned_imag = pltpu.roll(imag, HALF, 1)
        sendf[p, 0, pl.ds(k, ORB, stride=HERE), :] = jnp.where(low_half, real, turned_imag)
        sendf[p, 1, pl.ds(k, ORB, stride=HERE), :] = jnp.where(low_half, turned_real, imag)

    def forward_copy(p, target, plane):
        return pltpu.make_async_remote_copy(
            src_ref=sendf.at[p, lax.rem(target, 2), pl.ds((target // 2) * HERE, HERE), :],
            dst_ref=fbuf.at[p, pl.ds((core * CHIPS + chip) * HERE, HERE), :],
            send_sem=f_send.at[p], recv_sem=f_recv.at[p],
            device_id={"mom": target * 2 + core, "tm": plane}, device_id_type=MESH,
        )

    def back_copy(p, target):
        return pltpu.make_async_remote_copy(
            src_ref=sendb.at[p, target],
            dst_ref=rbuf.at[p, half, pl.ds(row * 8, 8), :],
            send_sem=b_send.at[p], recv_sem=b_recv.at[p],
            device_id={"mom": target * 2 + core, "tm": x}, device_id_type=MESH,
        )

    def pair_copy(p):
        block = fbuf.at[p, pl.ds(core * CHIPS * HERE, CHIPS * HERE), :]
        return pltpu.make_async_remote_copy(
            src_ref=block, dst_ref=block, send_sem=s_send.at[p], recv_sem=s_recv.at[p],
            device_id={"mom": chip * 2 + 1 - core, "tm": x}, device_id_type=MESH,
        )

    def arrived(p, k):
        columns = []
        for lp in range(2):
            first = rbuf[p, 0, pl.ds(lp * HERE + k, ORB, stride=8), :]
            second = rbuf[p, 1, pl.ds(lp * HERE + k, ORB, stride=8), :]
            real = jnp.where(low_half, first, pltpu.roll(second, HALF, 1))
            imag = jnp.where(low_half, pltpu.roll(first, HALF, 1), second)
            columns.append(jnp.concatenate([real, imag], axis=0))
        high, low = split(jnp.concatenate(columns, axis=1))
        return jnp.concatenate([high, low], axis=0)

    def collide(stack, slot):
        rows = 2 * ORB
        product = mm(stack, hank[slot, 0])
        total = product[:rows] + product[rows:] + mm(stack[:rows], hank[slot, 1])
        real = total[:ORB, :LANES] - total[ORB:, LANES:]
        imag = total[:ORB, LANES:] + total[ORB:, :LANES]
        return real, imag

    def own_forward(p):
        return pltpu.make_async_copy(
            sendf.at[p, half, pl.ds(row * HERE, HERE), :],
            fbuf.at[p, pl.ds((core * CHIPS + chip) * HERE, HERE), :],
            f_own.at[p],
        )

    def send_forward(p):
        own_forward(p).start()
        for dz, dy in OFFSETS:
            target = peer_chip(dz, dy)
            if p == PASSES - 1:
                for plane in (1, 0, 2):
                    forward_copy(p, target, plane).start()
            if dz or dy:
                forward_copy(p, target, last).start()

    def wait_forward(p):
        own_forward(p).wait()
        wait_rows(others * HERE, f_recv.at[p])

    def wait_rows(rows, sem):
        while rows:
            some = fbuf.at[0, pl.ds(0, min(rows, KX * KY)), :]
            pltpu.make_async_copy(some, some, sem).wait()
            rows -= min(rows, KX * KY)

    def start_block(block):
        for k in range(HERE):
            real, imag = propagate(k, hlv, (block + 1) * LANES, LANES)
            at = pl.ds(block * LANES, LANES)
            startv[0, k, :, at] = real
            startv[1, k, :, at] = imag

    def build_blocks(blocks):
        @pl.loop(0, HERE)
        def _(k):
            for block in blocks:
                build(k, block * HERE + k, hrv, hlv, block * LANES)

    def ahead_part(p, which):
        here = fbuf[p, pl.ds(pl.multiple_of(which * (CHIPS * HERE), CHIPS * HERE), CHIPS * HERE), :]
        high, low = split(jnp.concatenate([here, pltpu.roll(here, HALF, 1) * sign], axis=0))
        both = mm(ahead[which, 0], jnp.concatenate([high, low], axis=1))
        return both[:, :LANES] + both[:, LANES:] + mm(ahead[which, 1], high)

    def real_space(p):
        pair_copy(p).start()
        pos = ahead_part(p, core)
        pair_copy(p).wait_recv()
        pos = pos + ahead_part(p, 1 - core)
        turned = pltpu.roll(pos, HALF, 1)
        square = pos * pos
        turned_square = pltpu.roll(square, HALF, 1)
        lesser = (strength * (square + turned_square) + mf_term) * pos
        pair = strength * jnp.where(low_half, square - turned_square, 2.0 * pos * turned)
        both = jnp.concatenate([lesser, pair], axis=1)
        other = jnp.concatenate(
            [pltpu.roll(lesser, HALF, 1) * -sign, pltpu.roll(pair, HALF, 1) * -sign], axis=1
        )
        high, low = split(jnp.concatenate([both, other], axis=0))
        back = mm(backward[0], high) + mm(backward[0], low) + mm(backward[1], high)
        left = back[:, :LANES].reshape(CHIPS // 2, 8, LANES)
        right = back[:, LANES:].reshape(CHIPS // 2, 8, LANES)
        even = jnp.where(low_rows, left, pltpu.roll(right, 4, 1))
        odd = jnp.where(low_rows, pltpu.roll(left, 4, 1), right)
        for pair_index in range(CHIPS // 2):
            sendb[p, 2 * pair_index] = even[pair_index]
            sendb[p, 2 * pair_index + 1] = odd[pair_index]
        for dz, dy in OFFSETS[:-1]:
            back_copy(p, peer_chip(dz, dy)).start()
        rbuf[p, half, pl.ds(pl.multiple_of(row * 8, 8), 8), :] = sendb[p, chip]

    def wait_back(p):
        landed = sendb.at[p, pl.ds(0, others)]
        pltpu.make_async_copy(landed, landed, b_recv.at[p]).wait()

    for load in loads:
        load.wait()
    start_block(BLOCKS - 1)

    @pl.when(x == last)
    def _():
        newest_times = pl.ds((BLOCKS - 1) * LANES, LANES)
        for k in range(HERE):
            send_window(0, k, startv[0, k, :, newest_times], startv[1, k, :, newest_times])
        pl.semaphore_wait(barrier, others + 1 + (TM - 1) * CHIPS)
        send_forward(0)

    @pl.when(x < last)
    def _():
        pl.semaphore_wait(barrier, others + 2)
        for part in range(2):
            rim_copy(part).start()

    @pl.when(x == 0)
    def _():
        zeros = jnp.zeros((2, HERE, ORB, LANES), F32)
        hlv[:, :, :, pl.ds(0, LANES)] = zeros
        hrv[:, :, :, pl.ds(0, LANES)] = zeros

    build_blocks((BLOCKS - 1,))
    for block in range(BLOCKS - 1):
        start_block(block)

    @pl.when(x == last)
    def _():
        for p in range(PASSES - 1):
            if p:
                build_blocks((2,))
            wait_forward(p)
            real_space(p)
            if p == 0:
                build_blocks((1,))
            wait_back(p)
            for k in range(HERE):
                real, imag = collide(arrived(p, k), (BLOCKS - 1) * HERE + k)
                at = pl.ds((BLOCKS - 1) * LANES, LANES)
                send_window(p + 1, k, startv[0, k, :, at] + imag, startv[1, k, :, at] - real)
            send_forward(p + 1)

    @pl.when(x < last)
    def _():
        build_blocks((1, 2))

    @pl.when(x > 0)
    def _():
        for part in range(2):
            rim_copy(part).wait_recv()

    build_blocks((0,))

    p = PASSES - 1

    @pl.when(x == last)
    def _():
        wait_forward(p)

    @pl.when(x < last)
    def _():
        wait_rows(CHIPS * HERE, f_recv.at[p])

    real_space(p)
    wait_back(p)
    for k in range(HERE):
        stack = arrived(p, k)
        for block in range(BLOCKS):
            real, imag = collide(stack, block * HERE + k)
            at = pl.ds(block * LANES, LANES)
            out[0, k, :, at] = startv[0, k, :, at] + imag
            out[1, k, :, at] = startv[1, k, :, at] - real

    def sent_back(p):
        sent = sendb.at[p, pl.ds(0, others)]
        pltpu.make_async_copy(sent, sent, b_send.at[p]).wait()
        pair_copy(p).wait_send()

    sent_back(p)

    @pl.when(x == last)
    def _():
        for p in range(PASSES):
            wait_rows((others if p < PASSES - 1 else others + (TM - 1) * CHIPS) * HERE, f_send.at[p])
            if p < PASSES - 1:
                sent_back(p)

    @pl.when(x < last)
    def _():
        for part in range(2):
            rim_copy(part).wait_send()


def on_device(ahead, back, hist_lesser, hist_retarded, propagator, coupling, mf_weight, lag_weight):
    vmem = pl.BlockSpec(memory_space=pltpu.VMEM)
    hbm = pl.BlockSpec(memory_space=pltpu.HBM)
    padded = (2, HERE, ORB, (BLOCKS + 1) * LANES)
    return pl.pallas_call(
        kernel,
        out_shape=pltpu.VMEM(hist_lesser.shape, F32),
        in_specs=[hbm] * 8,
        out_specs=vmem,
        scratch_shapes=[
            pltpu.VMEM((2, HERE, ORB, ORB), F32),
            pltpu.SMEM((ORB * ORB,), F32),
            pltpu.SMEM((ORB * ORB,), F32),
            pltpu.SMEM((W,), F32),
            pltpu.VMEM(padded, F32),
            pltpu.VMEM(padded, F32),
            pltpu.VMEM((2, 2, KX * KY, KX * KY), BF16),
            pltpu.VMEM((2, CHIPS * HERE, 2 * KX * KY), BF16),
            pltpu.VMEM((2, HERE, ORB, BLOCKS * LANES), F32),
            pltpu.VMEM((BLOCKS * HERE, 2, 2 * LANES, 2 * LANES), BF16),
            pltpu.VMEM((PASSES, 2, ORB * HERE, LANES), F32),
            pltpu.VMEM((PASSES, KX * KY, LANES), F32),
            pltpu.VMEM((PASSES, CHIPS, 8, LANES), F32),
            pltpu.VMEM((PASSES, 2, ORB * 8, LANES), F32),
            pltpu.SemaphoreType.DMA((8,)),
            pltpu.SemaphoreType.DMA((2,)),
            pltpu.SemaphoreType.DMA((2,)),
            pltpu.SemaphoreType.DMA((PASSES,)),
            pltpu.SemaphoreType.DMA((PASSES,)),
            pltpu.SemaphoreType.DMA((PASSES,)),
            pltpu.SemaphoreType.DMA((PASSES,)),
            pltpu.SemaphoreType.DMA((PASSES,)),
            pltpu.SemaphoreType.DMA((PASSES,)),
            pltpu.SemaphoreType.DMA((PASSES,)),
        ],
        compiler_params=pltpu.CompilerParams(
            collective_id=0, has_side_effects=True, vmem_limit_bytes=67043328 - 4 * math.prod(hist_lesser.shape)
        ),
    )(hist_lesser, hist_retarded, propagator, coupling, mf_weight, lag_weight, ahead, back)


def solution(mesh):
    tables = momentum_tables()

    def step(*args):
        return jax.shard_map(
            on_device,
            mesh=mesh,
            in_specs=(
                P(None, None, None, None),
                P(None, None, None, None),
                P(None, "mom", None, "tm"),
                P(None, "mom", None, "tm"),
                P(None, "mom", None, None),
                P(),
                P(),
                P(),
            ),
            out_specs=P(None, "mom", None, "tm"),
            check_vma=False,
        )(*map(jnp.asarray, tables), *args)

    return step
```

time: 61.9 us -> 59.6 us (0.963)
  Pallas kernels: 59.8 us -> 58.8 us
  local copies, waits for them, and re-layouts: 1.67 us -> 0.71 us
    unnamed x1, local copies, waits for them, and re-layouts: 1.67 us -> 0.71 us
    pallas_call x1, Pallas kernels: 59.8 us -> 58.8 us  [on_device(): pl.pallas_call(kernel, out_shape=pltpu.VMEM(hist_lesser.shape, F32), in_s...]
where the time goes in v4:
time: 59.6 us; the launch traced here: 59.5 us
  Pallas kernels  58.8 us (99%)
  local copies, waits for them, and re-layouts  0.71 us (1%)
    pallas_call x1, Pallas kernels, on_device(): pl.pallas_call(kernel, out_shape=pltpu.VMEM(hist_lesser.shape, F32), in_s...  58.8 us

profile of v4, /device:TPU:1, one launch (start us, length us, event | category | flops | bytes accessed | tf_op | source)
XLA Modules:
  0.0 59.5 jit_solution(7032206064441632758)
XLA Ops:
  0.0 58.8 %shard_map.82 = f32[2,4,16,512]{3,2,1,0:T(8,128)S(1)} custom-call(f32[2,4,16,512]{3,2,1,0:T(8,128)} %hl.1, f32[2,4,16,512]{3,2,1,0:T(8,128)} %hr.1, f32[2,4,16,16]{3,2,1,0:T(8,128)} %prop_hbm.1, f32[256]{0:T(256)} %coup_hbm.1, f32[256]{0:T(256)} %mf_hbm.1, f32[8]{0:T(128)} %lag_hbm.1, bf16[2,2,256,256]{3,2,1,0:T(8,128)(2,1)} %constant.4.clone.ahead_hbm, ...), custom_call_target="tpu_custom_call" | custom-call | tf_op jit(solution)/shard_map/pallas_call | solution.py:404
  58.8 0.7 %copy.10 = f32[2,4,16,512]{3,2,1,0:T(8,128)} copy(f32[2,4,16,512]{3,2,1,0:T(8,128)S(1)} %shard_map.82) | data formatting | bytes 524288

commit v5 on v3

v5 whole, which is shorter than its diff:
```python
import math

import jax
import jax.numpy as jnp
import ml_dtypes
import numpy as np
from jax import lax
from jax.experimental import pallas as pl
from jax.experimental.pallas import tpu as pltpu
from jax.sharding import PartitionSpec as P

KX = 16
KY = 16
K = KX * KY
ORB = 16
W = 8
PASSES = 3
NZ, NY = 8, 4
CHIPS = NZ * NY
CORES = 2
TM = 4
HERE = 4
LANES = W * ORB
QUARTER = LANES // 4
HALF = LANES // 2
BLOCKS = 4

MESH = pl.DeviceIdType.MESH
F32 = jnp.float32
BF16 = jnp.bfloat16


def halves(full):
    full = full.astype(np.float32)
    high = full.astype(ml_dtypes.bfloat16)
    low = (full - high.astype(np.float32)).astype(ml_dtypes.bfloat16)
    return np.stack([high, low])


def momentum_tables():
    place = np.arange(K)

    def number(core, chip, here):
        return 8 * chip + 4 * core + here

    plain = number(place // 128, place // 4 % 32, place % 4)
    parted = number(place // 64 % 2, place // 2 % 32, place % 2 + 2 * (place // 128))

    def table(rows, columns):
        turn = (rows[:, None] // KY) * (columns[None, :] // KY) % KX
        turn = turn + (rows[:, None] % KY) * (columns[None, :] % KY) % KY
        phase = 2.0 * math.pi * turn / 16.0
        return halves(np.concatenate([np.cos(phase), np.sin(phase)], axis=1) / 16.0)

    return np.stack([table(plain, parted), table(plain, plain)])


def split(x):
    high = x.astype(BF16)
    return high, (x - high.astype(F32)).astype(BF16)


def mm(a, b):
    return jnp.dot(a, b, preferred_element_type=F32)


def ring(step, size):
    return min(step % size, -step % size)


PLACES = [
    (dz, dy, flip)
    for dz, dy in sorted(
        ((dz, dy) for dz in range(NZ) for dy in range(NY)), key=lambda o: -(ring(o[0], NZ) + ring(o[1], NY))
    )
    for flip in (1, 0)
]


def kernel(
    hl, hr, prop_hbm, coup_hbm, mf_hbm, lag_hbm, tables,
    out,
    prop, coup, mf, lag, hlv, hrv, tabs, startv, hank, sendf, fbuf, sendb, rbuf,
    load_sem, x_send, x_recv, f_send, f_recv, f_own, b_send, b_recv,
):
    dev = lax.axis_index("mom")
    x = lax.axis_index("tm")
    core = lax.rem(dev, CORES)
    chip = dev // CORES
    z = chip // NY
    y = lax.rem(chip, NY)
    last = TM - 1
    others = CHIPS * CORES - 1
    row = chip // 2
    quarter = lax.rem(chip, 2) * 2 + core
    slot_here = core * CHIPS + chip

    def at_place(place):
        dz, dy, flip = place
        return lax.rem(z + dz, NZ) * NY + lax.rem(y + dy, NY), 1 - core if flip else core

    def device(goal, cc, plane):
        return {"mom": goal * CORES + cc, "tm": plane}

    barrier = pltpu.get_barrier_semaphore()

    def greet(goal, cc, plane):
        pl.semaphore_signal(barrier, inc=1, device_id=device(goal, cc, plane), device_id_type=MESH)

    @pl.when(x < last)
    def _():
        for place in PLACES:
            greet(*at_place(place), last)

    for place in PLACES[:-1]:
        greet(*at_place(place), x)

    @pl.when(x > 0)
    def _():
        greet(chip, core, x - 1)

    small = [
        pltpu.make_async_copy(source, target, load_sem.at[4 + number])
        for number, (source, target) in enumerate(
            ((prop_hbm, prop), (coup_hbm, coup), (mf_hbm, mf), (lag_hbm, lag))
        )
    ]
    loads = [
        pltpu.make_async_copy(hl, hlv.at[:, :, :, pl.ds(LANES, BLOCKS * LANES)], load_sem.at[0]),
        pltpu.make_async_copy(hr, hrv.at[:, :, :, pl.ds(LANES, BLOCKS * LANES)], load_sem.at[1]),
    ]
    tables_in = pltpu.make_async_copy(tables, tabs, load_sem.at[2])

    for load in small + loads:
        load.start()
    tables_in.start()
    for load in small:
        load.wait()

    lane = lax.broadcasted_iota(jnp.int32, (1, LANES), 1)
    low_half = lane < HALF
    block_of_lane = lane // QUARTER
    first_of_two = lax.rem(block_of_lane, 2) == 0
    sign = jnp.where(first_of_two, -1.0, 1.0).astype(F32)

    coup_lane = jnp.zeros((1, LANES), F32)
    mf_lane = jnp.zeros((1, LANES), F32)
    for b in range(ORB):
        here = lax.rem(lane, ORB) == b
        coup_lane = jnp.where(here, coup[row * ORB + b], coup_lane)
        mf_lane = jnp.where(here, mf[row * ORB + b], mf_lane)
    strength = coup_lane * coup_lane
    newest = (lax.rem(lane, QUARTER) >= QUARTER - ORB) & (quarter == 3)
    mf_lane = jnp.where(newest, mf_lane, 0.0)
    first_row = lax.broadcasted_iota(jnp.int32, (K, 1), 0) == 0
    mf_term = jnp.where(first_row, mf_lane, 0.0)

    def turn(value):
        return jnp.where(
            first_of_two, pltpu.roll(value, LANES - QUARTER, 1), pltpu.roll(value, QUARTER, 1)
        )

    def transpose_blocks(parts):
        result = []
        for j in range(4):
            total = parts[j]
            for i in range(4):
                if i == j:
                    continue
                moved = pltpu.roll(parts[i], (QUARTER * (i - j)) % LANES, 1)
                total = jnp.where(block_of_lane == i, moved, total)
            result.append(total)
        return result

    def start_block(block):
        at = pl.ds(block * LANES, LANES)
        for k in range(HERE):
            stack = jnp.concatenate([prop[0, k], prop[1, k]], axis=0)
            real, imag = (
                jnp.dot(
                    stack, hlv[c, k, :, pl.ds((block + 1) * LANES, LANES)],
                    precision=lax.Precision.HIGHEST, preferred_element_type=F32,
                )
                for c in range(2)
            )
            startv[0, k, :, at] = real[:ORB] - imag[ORB:]
            startv[1, k, :, at] = real[ORB:] + imag[:ORB]

    def build(k, slot, source_r, source_l, lanes_from):
        for lp, source in enumerate((source_r, source_l)):
            for c in range(2):
                first = source[c, k, :, pl.ds(lanes_from, LANES)]
                second = source[c, k, :, pl.ds(lanes_from + LANES, LANES)]
                for m in range(W):
                    shift = ORB * (m + 1)
                    if shift < LANES:
                        moved = pltpu.roll(jnp.where(lane >= shift, first, second), LANES - shift, 1)
                    else:
                        moved = second
                    high, low = split(moved * lag[m])
                    at = lp * LANES + m * ORB
                    hank[slot, 0, pl.ds(at, ORB), pl.ds(c * LANES, LANES)] = high
                    hank[slot, 1, pl.ds(at, ORB), pl.ds(c * LANES, LANES)] = low

    def build_blocks(blocks):
        @pl.loop(0, HERE)
        def _(k):
            for block in blocks:
                build(k, block * HERE + k, hrv, hlv, block * LANES)

    def pack_window(p, reals, imags):
        for r in range(2):
            parts = transpose_blocks([reals[r], imags[r], reals[r + 2], imags[r + 2]])
            for w in range(4):
                sendf[p, w, pl.ds(r, ORB, stride=2), :] = parts[w]

    def forward_copy(p, place, plane):
        goal, cc = at_place(place)
        return pltpu.make_async_remote_copy(
            src_ref=sendf.at[p, lax.rem(goal, 2) * 2 + cc, pl.ds((goal // 2) * 2, 2), :],
            dst_ref=fbuf.at[p, pl.ds(slot_here * 2, 2), :],
            send_sem=f_send.at[p], recv_sem=f_recv.at[p],
            device_id=device(goal, cc, plane), device_id_type=MESH,
        )

    def own_forward(p):
        return pltpu.make_async_copy(
            sendf.at[p, quarter, pl.ds(row * 2, 2), :],
            fbuf.at[p, pl.ds(slot_here * 2, 2), :],
            f_own.at[p],
        )

    def back_copy(p, place):
        goal, cc = at_place(place)
        return pltpu.make_async_remote_copy(
            src_ref=sendb.at[p, pl.ds((cc * CHIPS + goal) * HERE, HERE), :],
            dst_ref=rbuf.at[p, quarter, pl.ds(row * HERE, HERE), :],
            send_sem=b_send.at[p], recv_sem=b_recv.at[p],
            device_id=device(goal, cc, x), device_id_type=MESH,
        )

    def own_back(p):
        return pltpu.make_async_copy(
            sendb.at[p, pl.ds(slot_here * HERE, HERE), :],
            rbuf.at[p, quarter, pl.ds(row * HERE, HERE), :],
            f_own.at[PASSES + p],
        )

    def wait_rows(rows, sem):
        while rows:
            some = sendb.at[0, pl.ds(0, min(rows, K)), :]
            pltpu.make_async_copy(some, some, sem).wait()
            rows -= min(rows, K)

    def send_forward(p):
        if p == PASSES - 1:
            for plane in range(last):
                for place in PLACES:
                    forward_copy(p, place, plane).start()
        own_forward(p).start()
        for place in PLACES[:-1]:
            forward_copy(p, place, last).start()

    def wait_forward(p):
        own_forward(p).wait()
        wait_rows(others * 2, f_recv.at[p])

    def real_space(p):
        here = fbuf[p]
        both = jnp.concatenate([here, turn(here) * sign], axis=0)
        high = both.astype(BF16).astype(F32)
        low = both - high
        front = jnp.where(low_half, high, pltpu.roll(low, HALF, 1)).astype(BF16)
        rear = jnp.where(low_half, pltpu.roll(high, HALF, 1), low).astype(BF16)
        count = K // 2
        stack = jnp.concatenate([front[:count], rear[:count], front[count:], rear[count:]], axis=0)
        main = mm(tabs[0, 0], stack)
        rest = mm(tabs[0, 1], stack)
        pos = main + pltpu.roll(main, HALF, 1) + jnp.where(low_half, rest, pltpu.roll(rest, HALF, 1))
        turned = turn(pos)
        square = pos * pos
        turned_square = turned * turned
        lesser = (strength * (square + turned_square) + mf_term) * pos
        pair = strength * jnp.where(first_of_two, square - turned_square, 2.0 * pos * turned)
        both = jnp.where(low_half, lesser, pair)
        high, low = split(jnp.concatenate([both, turn(both) * -sign], axis=0))
        main = mm(tabs[1, 0], jnp.concatenate([high, low], axis=1))
        sendb[p] = main[:, :LANES] + main[:, LANES:] + mm(tabs[1, 1], high)

    def send_back(p):
        own_back(p).start()
        for place in PLACES[:-1]:
            back_copy(p, place).start()

    def wait_back(p):
        own_back(p).wait()
        wait_rows(others * HERE, b_recv.at[p])

    def arrived(p, k):
        parts = transpose_blocks([rbuf[p, w, pl.ds(k, ORB, stride=HERE), :] for w in range(4)])
        lesser_real, lesser_imag, pair_real, pair_imag = parts
        high, low = split(
            jnp.concatenate(
                [
                    jnp.concatenate([lesser_real, pair_real], axis=1),
                    jnp.concatenate([lesser_imag, pair_imag], axis=1),
                ],
                axis=0,
            )
        )
        return jnp.concatenate([high, low], axis=0)

    def collide(stack, slot):
        rows = 2 * ORB
        product = mm(stack, hank[slot, 0])
        total = product[:rows] + product[rows:] + mm(stack[:rows], hank[slot, 1])
        real = total[:ORB, :LANES] - total[ORB:, LANES:]
        imag = total[:ORB, LANES:] + total[ORB:, :LANES]
        return real, imag

    def rim_copy(part):
        src, dst = ((hl, hlv), (hr, hrv))[part]
        return pltpu.make_async_remote_copy(
            src_ref=src.at[:, :, :, pl.ds((BLOCKS - 1) * LANES, LANES)],
            dst_ref=dst.at[:, :, :, pl.ds(0, LANES)],
            send_sem=x_send.at[part], recv_sem=x_recv.at[part],
            device_id=device(chip, core, lax.rem(x + 1, TM)), device_id_type=MESH,
        )

    for load in loads:
        load.wait()
    start_block(BLOCKS - 1)
    newest_times = pl.ds((BLOCKS - 1) * LANES, LANES)

    @pl.when(x == last)
    def _():
        pack_window(0, *([startv[c, k, :, newest_times] for k in range(HERE)] for c in range(2)))
        pl.semaphore_wait(barrier, others + last * (others + 1))
        send_forward(0)

    @pl.when(x < last)
    def _():
        pl.semaphore_wait(barrier, others + 1)
        for part in range(2):
            rim_copy(part).start()

    @pl.when(x == 0)
    def _():
        zeros = jnp.zeros((2, HERE, ORB, LANES), F32)
        hlv[:, :, :, pl.ds(0, LANES)] = zeros
        hrv[:, :, :, pl.ds(0, LANES)] = zeros

    build_blocks((BLOCKS - 1,))
    for block in range(BLOCKS - 1):
        start_block(block)
    tables_in.wait()

    @pl.when(x == last)
    def _():
        for p in range(PASSES - 1):
            if p:
                build_blocks((2,))
            wait_forward(p)
            real_space(p)
            send_back(p)
            if p == 0:
                build_blocks((1,))
            wait_back(p)
            reals, imags = [], []
            for k in range(HERE):
                real, imag = collide(arrived(p, k), (BLOCKS - 1) * HERE + k)
                reals.append(startv[0, k, :, newest_times] + imag)
                imags.append(startv[1, k, :, newest_times] - real)
            pack_window(p + 1, reals, imags)
            send_forward(p + 1)

    @pl.when(x < last)
    def _():
        build_blocks((1, 2))

    @pl.when(x > 0)
    def _():
        for part in range(2):
            rim_copy(part).wait_recv()

    build_blocks((0,))

    p = PASSES - 1

    @pl.when(x == last)
    def _():
        wait_forward(p)

    @pl.when(x < last)
    def _():
        wait_rows((others + 1) * 2, f_recv.at[p])

    real_space(p)
    send_back(p)
    wait_back(p)
    for k in range(HERE):
        stack = arrived(p, k)
        for block in range(BLOCKS):
            real, imag = collide(stack, block * HERE + k)
            at = pl.ds(block * LANES, LANES)
            out[0, k, :, at] = startv[0, k, :, at] + imag
            out[1, k, :, at] = startv[1, k, :, at] - real

    wait_rows(others * HERE, b_send.at[p])

    @pl.when(x == last)
    def _():
        for p in range(PASSES - 1):
            wait_rows(others * HERE, b_send.at[p])
            wait_rows(others * 2, f_send.at[p])
        wait_rows((others + last * (others + 1)) * 2, f_send.at[PASSES - 1])

    @pl.when(x < last)
    def _():
        for part in range(2):
            rim_copy(part).wait_send()


def on_device(tables, hist_lesser, hist_retarded, propagator, coupling, mf_weight, lag_weight):
    vmem = pl.BlockSpec(memory_space=pltpu.VMEM)
    hbm = pl.BlockSpec(memory_space=pltpu.HBM)
    padded = (2, HERE, ORB, (BLOCKS + 1) * LANES)
    return pl.pallas_call(
        kernel,
        out_shape=pltpu.VMEM(hist_lesser.shape, F32),
        in_specs=[hbm] * 7,
        out_specs=vmem,
        scratch_shapes=[
            pltpu.VMEM((2, HERE, ORB, ORB), F32),
            pltpu.SMEM((ORB * ORB,), F32),
            pltpu.SMEM((ORB * ORB,), F32),
            pltpu.SMEM((W,), F32),
            pltpu.VMEM(padded, F32),
            pltpu.VMEM(padded, F32),
            pltpu.VMEM((2, 2, K, 2 * K), BF16),
            pltpu.VMEM((2, HERE, ORB, BLOCKS * LANES), F32),
            pltpu.VMEM((BLOCKS * HERE, 2, 2 * LANES, 2 * LANES), BF16),
            pltpu.VMEM((PASSES, 4, 2 * ORB, LANES), F32),
            pltpu.VMEM((PASSES, K // 2, LANES), F32),
            pltpu.VMEM((PASSES, K, LANES), F32),
            pltpu.VMEM((PASSES, 4, HERE * ORB, LANES), F32),
            pltpu.SemaphoreType.DMA((8,)),
            pltpu.SemaphoreType.DMA((2,)),
            pltpu.SemaphoreType.DMA((2,)),
            pltpu.SemaphoreType.DMA((PASSES,)),
            pltpu.SemaphoreType.DMA((PASSES,)),
            pltpu.SemaphoreType.DMA((2 * PASSES,)),
            pltpu.SemaphoreType.DMA((PASSES,)),
            pltpu.SemaphoreType.DMA((PASSES,)),
        ],
        compiler_params=pltpu.CompilerParams(
            collective_id=0, has_side_effects=True, vmem_limit_bytes=67043328 - 4 * math.prod(hist_lesser.shape)
        ),
    )(hist_lesser, hist_retarded, propagator, coupling, mf_weight, lag_weight, tables)


def solution(mesh):
    tables = momentum_tables()

    def step(*args):
        return jax.shard_map(
            on_device,
            mesh=mesh,
            in_specs=(
                P(None, None, None, None),
                P(None, "mom", None, "tm"),
                P(None, "mom", None, "tm"),
                P(None, "mom", None, None),
                P(),
                P(),
                P(),
            ),
            out_specs=P(None, "mom", None, "tm"),
            check_vma=False,
        )(jnp.asarray(tables), *args)

    return step
```

time: 62.8 us -> 56.3 us (0.90)
  Pallas kernels: 61 us -> 55.1 us
  local copies, waits for them, and re-layouts: 1.67 us -> 0.71 us
    pallas_call x1, Pallas kernels: 61 us -> 55.1 us  [on_device(): pl.pallas_call(kernel, out_shape=pltpu.VMEM(hist_lesser.shape, F32), in_s...]
    unnamed x1, local copies, waits for them, and re-layouts: 1.67 us -> 0.71 us
where the time goes in v5:
time: 56.3 us; the launch traced here: 55.9 us
  Pallas kernels  55.1 us (98%)
  local copies, waits for them, and re-layouts  0.71 us (1%)
    pallas_call x1, Pallas kernels, on_device(): pl.pallas_call(kernel, out_shape=pltpu.VMEM(hist_lesser.shape, F32), in_s...  55.1 us

profile of v5, /device:TPU:1, one launch (start us, length us, event | category | flops | bytes accessed | tf_op | source)
XLA Modules:
  0.0 55.9 jit_solution(17002203278385123230)
XLA Ops:
  0.0 55.1 %shard_map.73 = f32[2,4,16,512]{3,2,1,0:T(8,128)S(1)} custom-call(f32[2,4,16,512]{3,2,1,0:T(8,128)} %hl.1, f32[2,4,16,512]{3,2,1,0:T(8,128)} %hr.1, f32[2,4,16,16]{3,2,1,0:T(8,128)} %prop_hbm.1, f32[256]{0:T(256)} %coup_hbm.1, f32[256]{0:T(256)} %mf_hbm.1, f32[8]{0:T(128)} %lag_hbm.1, bf16[2,2,256,512]{3,2,1,0:T(8,128)(2,1)} %constant.2.clone.tables), custom_call_target="tpu_custom_call" | custom-call | tf_op jit(solution)/shard_map/pallas_call | solution.py:428
  55.2 0.7 %copy.9 = f32[2,4,16,512]{3,2,1,0:T(8,128)} copy(f32[2,4,16,512]{3,2,1,0:T(8,128)S(1)} %shard_map.73) | data formatting | bytes 524288

commit v6 on v5

--- a/solution.py
+++ b/solution.py
@@ -30,29 +30,33 @@
 BF16 = jnp.bfloat16
 
 
-def halves(full):
-    full = full.astype(np.float32)
-    high = full.astype(ml_dtypes.bfloat16)
-    low = (full - high.astype(np.float32)).astype(ml_dtypes.bfloat16)
-    return np.stack([high, low])
+PAIRS = K // 2 - 2
 
 
 def momentum_tables():
     place = np.arange(K)
-
-    def number(core, chip, here):
-        return 8 * chip + 4 * core + here
-
-    plain = number(place // 128, place // 4 % 32, place % 4)
-    parted = number(place // 64 % 2, place // 2 % 32, place % 2 + 2 * (place // 128))
-
-    def table(rows, columns):
+    parted = 4 * (place // 2 % (K // 4)) + place % 2 + 2 * (place // (K // 2))
+    minus = (-(place // KY)) % KX * KY + (-(place % KY)) % KY
+    alone = place[minus == place]
+    upper = place[place < minus]
+
+    def waves(rows, columns):
         turn = (rows[:, None] // KY) * (columns[None, :] // KY) % KX
         turn = turn + (rows[:, None] % KY) * (columns[None, :] % KY) % KY
         phase = 2.0 * math.pi * turn / 16.0
-        return halves(np.concatenate([np.cos(phase), np.sin(phase)], axis=1) / 16.0)
-
-    return np.stack([table(plain, parted), table(plain, plain)])
+        return np.cos(phase) / 16.0, np.sin(phase) / 16.0
+
+    def table(momenta):
+        cosine, sine = waves(upper, momenta)
+        lone = waves(alone, momenta)[0]
+        return np.concatenate([cosine, lone[:2], sine, lone[2:]], axis=0).astype(np.float32)
+
+    def parts(full):
+        high = full.astype(ml_dtypes.bfloat16)
+        low = (full - high.astype(np.float32)).astype(ml_dtypes.bfloat16)
+        return np.stack([high, low])
+
+    return parts(table(parted).T), parts(table(place))
 
 
 def split(x):
@@ -78,9 +82,9 @@
 
 
 def kernel(
-    hl, hr, prop_hbm, coup_hbm, mf_hbm, lag_hbm, tables,
+    hl, hr, prop_hbm, coup_hbm, mf_hbm, lag_hbm, ahead_hbm, back_hbm,
     out,
-    prop, coup, mf, lag, hlv, hrv, tabs, startv, hank, sendf, fbuf, sendb, rbuf,
+    prop, coup, mf, lag, hlv, hrv, ahead, backward, startv, hank, sendf, fbuf, sendb, rbuf,
     load_sem, x_send, x_recv, f_send, f_recv, f_own, b_send, b_recv,
 ):
     dev = lax.axis_index("mom")
@@ -93,31 +97,16 @@
     others = CHIPS * CORES - 1
     row = chip // 2
     quarter = lax.rem(chip, 2) * 2 + core
-    slot_here = core * CHIPS + chip
+    far_z = [lax.rem(z + dz, NZ) * (NY * CORES) for dz in range(NZ)]
+    far_y = [lax.rem(y + dy, NY) * CORES for dy in range(NY)]
+    far_core = [core, 1 - core]
 
     def at_place(place):
         dz, dy, flip = place
-        return lax.rem(z + dz, NZ) * NY + lax.rem(y + dy, NY), 1 - core if flip else core
-
-    def device(goal, cc, plane):
-        return {"mom": goal * CORES + cc, "tm": plane}
-
-    barrier = pltpu.get_barrier_semaphore()
-
-    def greet(goal, cc, plane):
-        pl.semaphore_signal(barrier, inc=1, device_id=device(goal, cc, plane), device_id_type=MESH)
-
-    @pl.when(x < last)
-    def _():
-        for place in PLACES:
-            greet(*at_place(place), last)
-
-    for place in PLACES[:-1]:
-        greet(*at_place(place), x)
-
-    @pl.when(x > 0)
-    def _():
-        greet(chip, core, x - 1)
+        return far_z[dz] + far_y[dy] + far_core[flip]
+
+    def device(goal, plane):
+        return {"mom": goal, "tm": plane}
 
     small = [
         pltpu.make_async_copy(source, target, load_sem.at[4 + number])
@@ -129,36 +118,47 @@
         pltpu.make_async_copy(hl, hlv.at[:, :, :, pl.ds(LANES, BLOCKS * LANES)], load_sem.at[0]),
         pltpu.make_async_copy(hr, hrv.at[:, :, :, pl.ds(LANES, BLOCKS * LANES)], load_sem.at[1]),
     ]
-    tables_in = pltpu.make_async_copy(tables, tabs, load_sem.at[2])
-
-    for load in small + loads:
+    tables_in = [
+        pltpu.make_async_copy(ahead_hbm, ahead, load_sem.at[2]),
+        pltpu.make_async_copy(back_hbm, backward, load_sem.at[3]),
+    ]
+
+    for load in small + loads + tables_in:
         load.start()
-    tables_in.start()
+    barrier = pltpu.get_barrier_semaphore()
+
+    def greet(goal, plane):
+        pl.semaphore_signal(barrier, inc=1, device_id=device(goal, plane), device_id_type=MESH)
+
+    @pl.when(x < last)
+    def _():
+        for place in PLACES:
+            greet(at_place(place), last)
+
+    for place in PLACES[:-1]:
+        greet(at_place(place), x)
+
+    @pl.when(x > 0)
+    def _():
+        greet(dev, x - 1)
+
     for load in small:
         load.wait()
 
     lane = lax.broadcasted_iota(jnp.int32, (1, LANES), 1)
-    low_half = lane < HALF
     block_of_lane = lane // QUARTER
-    first_of_two = lax.rem(block_of_lane, 2) == 0
-    sign = jnp.where(first_of_two, -1.0, 1.0).astype(F32)
-
-    coup_lane = jnp.zeros((1, LANES), F32)
-    mf_lane = jnp.zeros((1, LANES), F32)
+
+    column = lax.broadcasted_iota(jnp.int32, (QUARTER, K), 0)
+    point = lax.broadcasted_iota(jnp.int32, (QUARTER, K), 1)
+    strength = jnp.zeros((QUARTER, K), F32)
+    mf_term = jnp.zeros((QUARTER, K), F32)
     for b in range(ORB):
-        here = lax.rem(lane, ORB) == b
-        coup_lane = jnp.where(here, coup[row * ORB + b], coup_lane)
-        mf_lane = jnp.where(here, mf[row * ORB + b], mf_lane)
-    strength = coup_lane * coup_lane
-    newest = (lax.rem(lane, QUARTER) >= QUARTER - ORB) & (quarter == 3)
-    mf_lane = jnp.where(newest, mf_lane, 0.0)
-    first_row = lax.broadcasted_iota(jnp.int32, (K, 1), 0) == 0
-    mf_term = jnp.where(first_row, mf_lane, 0.0)
-
-    def turn(value):
-        return jnp.where(
-            first_of_two, pltpu.roll(value, LANES - QUARTER, 1), pltpu.roll(value, QUARTER, 1)
-        )
+        here = lax.rem(column, ORB) == b
+        strength = jnp.where(here, coup[row * ORB + b], strength)
+        mf_term = jnp.where(here, mf[row * ORB + b], mf_term)
+    strength = strength * strength
+    mf_term = jnp.where((point == PAIRS) & (column >= ORB) & (quarter == 3), mf_term, 0.0)
+    lone = lane >= PAIRS
 
     def transpose_blocks(parts):
         result = []
@@ -212,39 +212,31 @@
         for r in range(2):
             parts = transpose_blocks([reals[r], imags[r], reals[r + 2], imags[r + 2]])
             for w in range(4):
-                sendf[p, w, pl.ds(r, ORB, stride=2), :] = parts[w]
+                sendf[p, pl.ds(2 * w + r, ORB, stride=8), :] = parts[w]
 
     def forward_copy(p, place, plane):
-        goal, cc = at_place(place)
+        goal = at_place(place)
         return pltpu.make_async_remote_copy(
-            src_ref=sendf.at[p, lax.rem(goal, 2) * 2 + cc, pl.ds((goal // 2) * 2, 2), :],
-            dst_ref=fbuf.at[p, pl.ds(slot_here * 2, 2), :],
+            src_ref=sendf.at[p, pl.ds(goal * 2, 2), :], dst_ref=fbuf.at[p, pl.ds(dev * 2, 2), :],
             send_sem=f_send.at[p], recv_sem=f_recv.at[p],
-            device_id=device(goal, cc, plane), device_id_type=MESH,
+            device_id=device(goal, plane), device_id_type=MESH,
         )
 
     def own_forward(p):
-        return pltpu.make_async_copy(
-            sendf.at[p, quarter, pl.ds(row * 2, 2), :],
-            fbuf.at[p, pl.ds(slot_here * 2, 2), :],
-            f_own.at[p],
-        )
+        here = pl.ds(dev * 2, 2)
+        return pltpu.make_async_copy(sendf.at[p, here, :], fbuf.at[p, here, :], f_own.at[p])
 
     def back_copy(p, place):
-        goal, cc = at_place(place)
+        goal = at_place(place)
         return pltpu.make_async_remote_copy(
-            src_ref=sendb.at[p, pl.ds((cc * CHIPS + goal) * HERE, HERE), :],
-            dst_ref=rbuf.at[p, quarter, pl.ds(row * HERE, HERE), :],
+            src_ref=sendb.at[p, pl.ds(goal * HERE, HERE), :], dst_ref=rbuf.at[p, pl.ds(dev * HERE, HERE), :],
             send_sem=b_send.at[p], recv_sem=b_recv.at[p],
-            device_id=device(goal, cc, x), device_id_type=MESH,
+            device_id=device(goal, x), device_id_type=MESH,
         )
 
     def own_back(p):
-        return pltpu.make_async_copy(
-            sendb.at[p, pl.ds(slot_here * HERE, HERE), :],
-            rbuf.at[p, quarter, pl.ds(row * HERE, HERE), :],
-            f_own.at[PASSES + p],
-        )
+        here = pl.ds(dev * HERE, HERE)
+        return pltpu.make_async_copy(sendb.at[p, here, :], rbuf.at[p, here, :], f_own.at[PASSES + p])
 
     def wait_rows(rows, sem):
         while rows:
@@ -266,26 +258,43 @@
         wait_rows(others * 2, f_recv.at[p])
 
     def real_space(p):
-        here = fbuf[p]
-        both = jnp.concatenate([here, turn(here) * sign], axis=0)
-        high = both.astype(BF16).astype(F32)
-        low = both - high
-        front = jnp.where(low_half, high, pltpu.roll(low, HALF, 1)).astype(BF16)
-        rear = jnp.where(low_half, pltpu.roll(high, HALF, 1), low).astype(BF16)
-        count = K // 2
-        stack = jnp.concatenate([front[:count], rear[:count], front[count:], rear[count:]], axis=0)
-        main = mm(tabs[0, 0], stack)
-        rest = mm(tabs[0, 1], stack)
-        pos = main + pltpu.roll(main, HALF, 1) + jnp.where(low_half, rest, pltpu.roll(rest, HALF, 1))
-        turned = turn(pos)
-        square = pos * pos
-        turned_square = turned * turned
-        lesser = (strength * (square + turned_square) + mf_term) * pos
-        pair = strength * jnp.where(first_of_two, square - turned_square, 2.0 * pos * turned)
-        both = jnp.where(low_half, lesser, pair)
-        high, low = split(jnp.concatenate([both, turn(both) * -sign], axis=0))
-        main = mm(tabs[1, 0], jnp.concatenate([high, low], axis=1))
-        sendb[p] = main[:, :LANES] + main[:, LANES:] + mm(tabs[1, 1], high)
+        turned = fbuf[p].T
+        value = jnp.concatenate([turned[:HALF], turned[HALF:]], axis=1)
+        high, low = split(value)
+        product = mm(jnp.concatenate([high, low], axis=0), ahead[0])
+        product = product[:HALF] + product[HALF:] + mm(high, ahead[1])
+        even, odd = product[:, :LANES], product[:, LANES:]
+        crossed = jnp.concatenate([-odd[QUARTER:], odd[:QUARTER]], axis=0)
+        pos = jnp.concatenate(
+            [jnp.where(lone, even, even + crossed), jnp.where(lone, odd, even - crossed)], axis=1
+        )
+        real, imag = pos[:QUARTER], pos[QUARTER:]
+        square_real, square_imag = real * real, imag * imag
+        factor = strength * (square_real + square_imag) + mf_term
+        twice = 2.0 * strength
+        both = jnp.concatenate(
+            [factor * real, factor * imag, strength * (square_real - square_imag), twice * real * imag],
+            axis=0,
+        )
+        first, second = both[:, :LANES], both[:, LANES:]
+        change = first - second
+        crossed = jnp.concatenate(
+            [
+                change[QUARTER : 2 * QUARTER],
+                -change[:QUARTER],
+                change[3 * QUARTER :],
+                -change[2 * QUARTER : 3 * QUARTER],
+            ],
+            axis=0,
+        )
+        value = jnp.concatenate(
+            [jnp.where(lone, first, first + second), jnp.where(lone, second, crossed)], axis=1
+        )
+        high, low = split(value)
+        product = mm(jnp.concatenate([high, low], axis=0), backward[0])
+        product = product[:LANES] + product[LANES:] + mm(high, backward[1])
+        sendb[p, pl.ds(0, LANES), :] = product[:, :LANES].T
+        sendb[p, pl.ds(LANES, LANES), :] = product[:, LANES:].T
 
     def send_back(p):
         own_back(p).start()
@@ -297,7 +306,7 @@
         wait_rows(others * HERE, b_recv.at[p])
 
     def arrived(p, k):
-        parts = transpose_blocks([rbuf[p, w, pl.ds(k, ORB, stride=HERE), :] for w in range(4)])
+        parts = transpose_blocks([rbuf[p, pl.ds(w * HERE + k, ORB, stride=4 * HERE), :] for w in range(4)])
         lesser_real, lesser_imag, pair_real, pair_imag = parts
         high, low = split(
             jnp.concatenate(
@@ -324,7 +333,7 @@
             src_ref=src.at[:, :, :, pl.ds((BLOCKS - 1) * LANES, LANES)],
             dst_ref=dst.at[:, :, :, pl.ds(0, LANES)],
             send_sem=x_send.at[part], recv_sem=x_recv.at[part],
-            device_id=device(chip, core, lax.rem(x + 1, TM)), device_id_type=MESH,
+            device_id=device(dev, lax.rem(x + 1, TM)), device_id_type=MESH,
         )
 
     for load in loads:
@@ -353,7 +362,8 @@
     build_blocks((BLOCKS - 1,))
     for block in range(BLOCKS - 1):
         start_block(block)
-    tables_in.wait()
+    for load in tables_in:
+        load.wait()
 
     @pl.when(x == last)
     def _():
@@ -421,14 +431,14 @@
             rim_copy(part).wait_send()
 
 
-def on_device(tables, hist_lesser, hist_retarded, propagator, coupling, mf_weight, lag_weight):
+def on_device(ahead, back, hist_lesser, hist_retarded, propagator, coupling, mf_weight, lag_weight):
     vmem = pl.BlockSpec(memory_space=pltpu.VMEM)
     hbm = pl.BlockSpec(memory_space=pltpu.HBM)
     padded = (2, HERE, ORB, (BLOCKS + 1) * LANES)
     return pl.pallas_call(
         kernel,
         out_shape=pltpu.VMEM(hist_lesser.shape, F32),
-        in_specs=[hbm] * 7,
+        in_specs=[hbm] * 8,
         out_specs=vmem,
         scratch_shapes=[
             pltpu.VMEM((2, HERE, ORB, ORB), F32),
@@ -437,13 +447,14 @@
             pltpu.SMEM((W,), F32),
             pltpu.VMEM(padded, F32),
             pltpu.VMEM(padded, F32),
-            pltpu.VMEM((2, 2, K, 2 * K), BF16),
+            pltpu.VMEM((2, K, K), BF16),
+            pltpu.VMEM((2, K, K), BF16),
             pltpu.VMEM((2, HERE, ORB, BLOCKS * LANES), F32),
             pltpu.VMEM((BLOCKS * HERE, 2, 2 * LANES, 2 * LANES), BF16),
-            pltpu.VMEM((PASSES, 4, 2 * ORB, LANES), F32),
+            pltpu.VMEM((PASSES, K // 2, LANES), F32),
             pltpu.VMEM((PASSES, K // 2, LANES), F32),
             pltpu.VMEM((PASSES, K, LANES), F32),
-            pltpu.VMEM((PASSES, 4, HERE * ORB, LANES), F32),
+            pltpu.VMEM((PASSES, K, LANES), F32),
             pltpu.SemaphoreType.DMA((8,)),
             pltpu.SemaphoreType.DMA((2,)),
             pltpu.SemaphoreType.DMA((2,)),
@@ -456,7 +467,7 @@
         compiler_params=pltpu.CompilerParams(
             collective_id=0, has_side_effects=True, vmem_limit_bytes=67043328 - 4 * math.prod(hist_lesser.shape)
         ),
-    )(hist_lesser, hist_retarded, propagator, coupling, mf_weight, lag_weight, tables)
+    )(hist_lesser, hist_retarded, propagator, coupling, mf_weight, lag_weight, ahead, back)
 
 
 def solution(mesh):
@@ -467,7 +478,8 @@
             on_device,
             mesh=mesh,
             in_specs=(
-                P(None, None, None, None),
+                P(None, None, None),
+                P(None, None, None),
                 P(None, "mom", None, "tm"),
                 P(None, "mom", None, "tm"),
                 P(None, "mom", None, None),
@@ -477,6 +489,6 @@
             ),
             out_specs=P(None, "mom", None, "tm"),
             check_vma=False,
-        )(jnp.asarray(tables), *args)
+        )(*map(jnp.asarray, tables), *args)
 
     return step

time: 56.3 us -> 55.6 us (0.988)
  Pallas kernels: 55.1 us -> 54.1 us
    pallas_call x1, Pallas kernels: 55.1 us -> 54.1 us  [on_device(): pl.pallas_call(kernel, out_shape=pltpu.VMEM(hist_lesser.shape, F32), in_s...]
where the time goes in v6:
time: 55.6 us; the launch traced here: 54.8 us
  Pallas kernels  54.1 us (97%)
  local copies, waits for them, and re-layouts  0.71 us (1%)
    pallas_call x1, Pallas kernels, on_device(): pl.pallas_call(kernel, out_shape=pltpu.VMEM(hist_lesser.shape, F32), in_s...  54.1 us

profile of v6, /device:TPU:1, one launch (start us, length us, event | category | flops | bytes accessed | tf_op | source)
XLA Modules:
  0.0 54.8 jit_solution(7195064583228746173)
XLA Ops:
  0.0 54.1 %shard_map.82 = f32[2,4,16,512]{3,2,1,0:T(8,128)S(1)} custom-call(f32[2,4,16,512]{3,2,1,0:T(8,128)} %hl.1, f32[2,4,16,512]{3,2,1,0:T(8,128)} %hr.1, f32[2,4,16,16]{3,2,1,0:T(8,128)} %prop_hbm.1, f32[256]{0:T(256)} %coup_hbm.1, f32[256]{0:T(256)} %mf_hbm.1, f32[8]{0:T(128)} %lag_hbm.1, bf16[2,256,256]{2,1,0:T(8,128)(2,1)} %constant.4.clone.ahead_hbm, ...), custom_call_target="tpu_custom_call" | custom-call | tf_op jit(solution)/shard_map/pallas_call | solution.py:438
  54.1 0.7 %copy.10 = f32[2,4,16,512]{3,2,1,0:T(8,128)} copy(f32[2,4,16,512]{3,2,1,0:T(8,128)S(1)} %shard_map.82) | data formatting | bytes 524288

commit v7 on v6

--- a/solution.py
+++ b/solution.py
@@ -85,7 +85,7 @@
     hl, hr, prop_hbm, coup_hbm, mf_hbm, lag_hbm, ahead_hbm, back_hbm,
     out,
     prop, coup, mf, lag, hlv, hrv, ahead, backward, startv, hank, sendf, fbuf, sendb, rbuf,
-    load_sem, x_send, x_recv, f_send, f_recv, f_own, b_send, b_recv,
+    load_sem, x_send, x_recv, f_send, f_recv, f_own, b_send, b_recv, ready,
 ):
     dev = lax.axis_index("mom")
     x = lax.axis_index("tm")
@@ -130,17 +130,17 @@
     def greet(goal, plane):
         pl.semaphore_signal(barrier, inc=1, device_id=device(goal, plane), device_id_type=MESH)
 
-    @pl.when(x < last)
-    def _():
-        for place in PLACES:
-            greet(at_place(place), last)
-
     for place in PLACES[:-1]:
         greet(at_place(place), x)
 
     @pl.when(x > 0)
     def _():
         greet(dev, x - 1)
+
+    @pl.when(x == last)
+    def _():
+        for plane in range(last - 1):
+            greet(dev, plane)
 
     for load in small:
         load.wait()
@@ -246,6 +246,7 @@
 
     def send_forward(p):
         if p == PASSES - 1:
+            pl.semaphore_wait(ready, last)
             for plane in range(last):
                 for place in PLACES:
                     forward_copy(p, place, plane).start()
@@ -344,12 +345,20 @@
     @pl.when(x == last)
     def _():
         pack_window(0, *([startv[c, k, :, newest_times] for k in range(HERE)] for c in range(2)))
-        pl.semaphore_wait(barrier, others + last * (others + 1))
+        pl.semaphore_wait(barrier, others)
         send_forward(0)
 
+    @pl.when(x == last - 1)
+    def _():
+        pl.semaphore_wait(barrier, others + 1)
+
+    @pl.when(x < last - 1)
+    def _():
+        pl.semaphore_wait(barrier, others + 2)
+
     @pl.when(x < last)
     def _():
-        pl.semaphore_wait(barrier, others + 1)
+        pl.semaphore_signal(ready, inc=1, device_id=device(dev, last), device_id_type=MESH)
         for part in range(2):
             rim_copy(part).start()
 
@@ -463,6 +472,7 @@
             pltpu.SemaphoreType.DMA((2 * PASSES,)),
             pltpu.SemaphoreType.DMA((PASSES,)),
             pltpu.SemaphoreType.DMA((PASSES,)),
+            pltpu.SemaphoreType.REGULAR,
         ],
         compiler_params=pltpu.CompilerParams(
             collective_id=0, has_side_effects=True, vmem_limit_bytes=67043328 - 4 * math.prod(hist_lesser.shape)

time: 55.6 us -> 54.8 us (0.986)
  Pallas kernels: 54.1 us -> 53.1 us
    pallas_call x1, Pallas kernels: 54.1 us -> 53.1 us  [on_device(): pl.pallas_call(kernel, out_shape=pltpu.VMEM(hist_lesser.shape, F32), in_s...]
where the time goes in v7:
time: 54.8 us; the launch traced here: 53.9 us
  Pallas kernels  53.1 us (97%)
  local copies, waits for them, and re-layouts  0.71 us (1%)
    pallas_call x1, Pallas kernels, on_device(): pl.pallas_call(kernel, out_shape=pltpu.VMEM(hist_lesser.shape, F32), in_s...  53.1 us

profile of v7, /device:TPU:1, one launch (start us, length us, event | category | flops | bytes accessed | tf_op | source)
XLA Modules:
  0.0 53.9 jit_solution(5693629944058264526)
XLA Ops:
  0.0 53.1 %shard_map.82 = f32[2,4,16,512]{3,2,1,0:T(8,128)S(1)} custom-call(f32[2,4,16,512]{3,2,1,0:T(8,128)} %hl.1, f32[2,4,16,512]{3,2,1,0:T(8,128)} %hr.1, f32[2,4,16,16]{3,2,1,0:T(8,128)} %prop_hbm.1, f32[256]{0:T(256)} %coup_hbm.1, f32[256]{0:T(256)} %mf_hbm.1, f32[8]{0:T(128)} %lag_hbm.1, bf16[2,256,256]{2,1,0:T(8,128)(2,1)} %constant.4.clone.ahead_hbm, ...), custom_call_target="tpu_custom_call" | custom-call | tf_op jit(solution)/shard_map/pallas_call | solution.py:447
  53.1 0.7 %copy.10 = f32[2,4,16,512]{3,2,1,0:T(8,128)} copy(f32[2,4,16,512]{3,2,1,0:T(8,128)S(1)} %shard_map.82) | data formatting | bytes 524288

commit v8 on v7

--- a/solution.py
+++ b/solution.py
@@ -146,7 +146,8 @@
         load.wait()
 
     lane = lax.broadcasted_iota(jnp.int32, (1, LANES), 1)
-    block_of_lane = lane // QUARTER
+    low_half = lane < HALF
+    even_block = lax.rem(lane // QUARTER, 2) == 0
 
     column = lax.broadcasted_iota(jnp.int32, (QUARTER, K), 0)
     point = lax.broadcasted_iota(jnp.int32, (QUARTER, K), 1)
@@ -161,16 +162,20 @@
     lone = lane >= PAIRS
 
     def transpose_blocks(parts):
-        result = []
-        for j in range(4):
-            total = parts[j]
-            for i in range(4):
-                if i == j:
-                    continue
-                moved = pltpu.roll(parts[i], (QUARTER * (i - j)) % LANES, 1)
-                total = jnp.where(block_of_lane == i, moved, total)
-            result.append(total)
-        return result
+        def swap_halves(a, b):
+            moved = pltpu.roll(jnp.where(low_half, b, a), HALF, 1)
+            return jnp.where(low_half, a, moved), jnp.where(low_half, moved, b)
+
+        def swap_blocks(a, b):
+            moving = jnp.where(even_block, b, a)
+            moved = jnp.where(
+                even_block, pltpu.roll(moving, LANES - QUARTER, 1), pltpu.roll(moving, QUARTER, 1)
+            )
+            return jnp.where(even_block, a, moved), jnp.where(even_block, moved, b)
+
+        a, c = swap_halves(parts[0], parts[2])
+        b, d = swap_halves(parts[1], parts[3])
+        return [*swap_blocks(a, b), *swap_blocks(c, d)]
 
     def start_block(block):
         at = pl.ds(block * LANES, LANES)

time: 54.8 us -> 55.2 us (level)
  no operation moved by 1% of the time
where the time goes in v8:
time: 55.2 us; the launch traced here: 54.4 us
  Pallas kernels  53.6 us (97%)
  local copies, waits for them, and re-layouts  0.71 us (1%)
    pallas_call x1, Pallas kernels, on_device(): pl.pallas_call(kernel, out_shape=pltpu.VMEM(hist_lesser.shape, F32), in_s...  53.6 us

profile of v8, /device:TPU:1, one launch (start us, length us, event | category | flops | bytes accessed | tf_op | source)
XLA Modules:
  0.0 54.4 jit_solution(8018202484692529159)
XLA Ops:
  0.0 53.6 %shard_map.82 = f32[2,4,16,512]{3,2,1,0:T(8,128)S(1)} custom-call(f32[2,4,16,512]{3,2,1,0:T(8,128)} %hl.1, f32[2,4,16,512]{3,2,1,0:T(8,128)} %hr.1, f32[2,4,16,16]{3,2,1,0:T(8,128)} %prop_hbm.1, f32[256]{0:T(256)} %coup_hbm.1, f32[256]{0:T(256)} %mf_hbm.1, f32[8]{0:T(128)} %lag_hbm.1, bf16[2,256,256]{2,1,0:T(8,128)(2,1)} %constant.4.clone.ahead_hbm, ...), custom_call_target="tpu_custom_call" | custom-call | tf_op jit(solution)/shard_map/pallas_call | solution.py:452
  53.6 0.7 %copy.10 = f32[2,4,16,512]{3,2,1,0:T(8,128)} copy(f32[2,4,16,512]{3,2,1,0:T(8,128)S(1)} %shard_map.82) | data formatting | bytes 524288

commit v9 on v7

--- a/solution.py
+++ b/solution.py
@@ -108,6 +108,23 @@
     def device(goal, plane):
         return {"mom": goal, "tm": plane}
 
+    barrier = pltpu.get_barrier_semaphore()
+
+    def greet(goal, plane):
+        pl.semaphore_signal(barrier, inc=1, device_id=device(goal, plane), device_id_type=MESH)
+
+    for place in PLACES[:-1]:
+        greet(at_place(place), x)
+
+    @pl.when(x > 0)
+    def _():
+        greet(dev, x - 1)
+
+    @pl.when(x == last)
+    def _():
+        for plane in range(last - 1):
+            greet(dev, plane)
+
     small = [
         pltpu.make_async_copy(source, target, load_sem.at[4 + number])
         for number, (source, target) in enumerate(
@@ -125,23 +142,6 @@
 
     for load in small + loads + tables_in:
         load.start()
-    barrier = pltpu.get_barrier_semaphore()
-
-    def greet(goal, plane):
-        pl.semaphore_signal(barrier, inc=1, device_id=device(goal, plane), device_id_type=MESH)
-
-    for place in PLACES[:-1]:
-        greet(at_place(place), x)
-
-    @pl.when(x > 0)
-    def _():
-        greet(dev, x - 1)
-
-    @pl.when(x == last)
-    def _():
-        for plane in range(last - 1):
-            greet(dev, plane)
-
     for load in small:
         load.wait()
 

time: 54.8 us -> 54.8 us (level)
  no operation moved by 1% of the time
where the time goes in v9:
time: 54.8 us; the launch traced here: 53.9 us
  Pallas kernels  53.2 us (97%)
  local copies, waits for them, and re-layouts  0.71 us (1%)
    pallas_call x1, Pallas kernels, on_device(): pl.pallas_call(kernel, out_shape=pltpu.VMEM(hist_lesser.shape, F32), in_s...  53.2 us

profile of v9, /device:TPU:1, one launch (start us, length us, event | category | flops | bytes accessed | tf_op | source)
XLA Modules:
  0.0 53.9 jit_solution(10558731227247522878)
XLA Ops:
  0.0 53.2 %shard_map.82 = f32[2,4,16,512]{3,2,1,0:T(8,128)S(1)} custom-call(f32[2,4,16,512]{3,2,1,0:T(8,128)} %hl.1, f32[2,4,16,512]{3,2,1,0:T(8,128)} %hr.1, f32[2,4,16,16]{3,2,1,0:T(8,128)} %prop_hbm.1, f32[256]{0:T(256)} %coup_hbm.1, f32[256]{0:T(256)} %mf_hbm.1, f32[8]{0:T(128)} %lag_hbm.1, bf16[2,256,256]{2,1,0:T(8,128)(2,1)} %constant.4.clone.ahead_hbm, ...), custom_call_target="tpu_custom_call" | custom-call | tf_op jit(solution)/shard_map/pallas_call | solution.py:447
  53.2 0.7 %copy.10 = f32[2,4,16,512]{3,2,1,0:T(8,128)} copy(f32[2,4,16,512]{3,2,1,0:T(8,128)S(1)} %shard_map.82) | data formatting | bytes 524288
